TPU v7x, 128 devices: a whole 4x4x4 slice. The times are simulated.
128 devices in a mesh: row: 8 (over x, core), col: 16 (over z, y).
Axes of the slice: x: 4, y: 4, z: 4, core: 2. Of those that a mesh axis runs over, the one named last changes fastest.
Arguments:
- model_init: float32 [2, 2, 16, 16384], P(None, None, None, 'col'), may hold values from -2 to 2
- observed: float32 [2, 2, 16, 32768], P(None, None, None, ('row', 'col')), may hold values from -6 to 6
- left_bases: bfloat16 [128, 64, 2, 96, 2, 256], P(('row', 'col')), may hold values from -0.078125 to 0.078125
- right_bases: bfloat16 [128, 64, 2, 96, 2, 256], P('row', 'col'), may hold values from -0.078125 to 0.078125
- tile_ranks: int32 [128, 64, 2], P('row', 'col'), may hold values from 8 to 96
- gate_start: int32 [16, 32768], P(None, ('row', 'col')), may hold values from 0 to 31
- gate_stop: int32 [16, 32768], P(None, ('row', 'col')), may hold values from 32 to 64
Outputs:
- model_final: float32 [2, 2, 16, 16384], P(None, None, None, 'col')
- residual_final: float32 [2, 2, 16, 32768], P(None, None, None, ('row', 'col'))
All inputs are finite; a program needn't handle non-finite values.
Results may differ from a plain program's by a relative error of at most 0.009.
Values may be sent and summed in bfloat16 or wider, within the bound.
No kernel may reach another device: no remote copies, remote signals or barrier semaphores. Data moves between devices by JAX's collectives and lax.ppermute only.
A program may use at most 128 MiB of HBM per device.

v0:
```python
import math

import jax
import jax.numpy as jnp
from jax import lax
from jax.sharding import PartitionSpec as P

NV = 16
TILE = 256
RMAX = 96
F = 2
NT = 64
ITERS = 2


step_length = 0.8


def time_table(samples):
    sample_times = jnp.arange(samples, dtype=jnp.float32)[:, None]
    freq_bins = (3.0 + 5.0 * jnp.arange(F, dtype=jnp.float32))[None, :]
    phases = 2.0 * math.pi * sample_times * freq_bins / samples
    return jnp.concatenate([jnp.cos(phases), -jnp.sin(phases)], axis=1)


def apply_gate(field, gate_start, gate_stop):
    transform = time_table(NT)
    flattened = field.reshape(2 * F, -1)
    signal = jnp.dot(transform, flattened, precision=lax.Precision.HIGHEST)
    sample_index = jnp.arange(NT, dtype=jnp.int32)[:, None, None]
    window = ((sample_index >= gate_start[None]) & (sample_index < gate_stop[None])).astype(
        jnp.float32
    )
    windowed = signal * window.reshape(NT, -1)
    returned = jnp.dot(transform.T, windowed, precision=lax.Precision.HIGHEST) * (2.0 / NT)
    return returned.reshape(field.shape)


def pair_rows(field):
    real_part, imag_part = (field[0], field[1])
    upper_pair = jnp.stack([real_part, imag_part], axis=3)
    lower_pair = jnp.stack([imag_part, -real_part], axis=3)
    joined = jnp.stack([upper_pair, lower_pair], axis=1)
    return jnp.transpose(joined, (3, 0, 1, 2, 4, 5))


def combine(stacked):
    real_part = stacked[:, :, 0, :, 0] - stacked[:, :, 1, :, 1]
    imag_part = stacked[:, :, 0, :, 1] + stacked[:, :, 1, :, 0]
    joined = jnp.stack([real_part, imag_part], axis=0)
    joined = jnp.transpose(joined, (0, 2, 3, 1, 4))
    return joined.reshape(joined.shape[0], joined.shape[1], joined.shape[2], -1)


def forward(low_model, left_bases, right_bases, rank_keep):
    blocks = low_model.shape[3] // TILE
    paired = pair_rows(low_model.reshape(2, F, NV, blocks, TILE))
    coefficients = jnp.einsum(
        "jfavcs,ijfkcs->ijfavk", paired, right_bases, preferred_element_type=jnp.float32
    )
    coefficients = (coefficients * rank_keep[:, :, :, None, None, :]).astype(jnp.bfloat16)
    sendable = coefficients.reshape(coefficients.shape[0], coefficients.shape[1], F, 2, NV * RMAX)
    received = lax.all_to_all(sendable, "col", split_axis=0, concat_axis=1, tiled=True)
    received = received.reshape(received.shape[0], received.shape[1], F, 2, NV, RMAX)
    modeled = jnp.einsum(
        "ijfavk,ijfkcn->ifavcn", received, left_bases, preferred_element_type=jnp.float32
    )
    return combine(modeled)


def adjoint(residual, left_bases, right_bases, rank_keep):
    blocks = residual.shape[3] // TILE
    paired = pair_rows(residual.astype(jnp.bfloat16).reshape(2, F, NV, blocks, TILE))
    coefficients = jnp.einsum(
        "ifavcn,ijfkcn->ijfavk", paired, left_bases, preferred_element_type=jnp.float32
    )
    coefficients = coefficients.astype(jnp.bfloat16)
    sendable = coefficients.reshape(blocks, coefficients.shape[1], F, 2, NV * RMAX)
    received = lax.all_to_all(sendable, "col", split_axis=1, concat_axis=0, tiled=True)
    received = received.reshape(received.shape[0], received.shape[1], F, 2, NV, RMAX)
    received = received * rank_keep[:, :, :, None, None, :].astype(jnp.bfloat16)
    column_terms = jnp.einsum(
        "ijfavk,ijfkcs->jfavcs", received, right_bases, preferred_element_type=jnp.float32
    )
    return combine(column_terms)


def shards(model_init, observed, left_bases, right_bases, tile_ranks, gate_start, gate_stop):
    rank_index = jnp.arange(RMAX, dtype=jnp.int32)
    rank_keep = (rank_index < tile_ranks[..., None]).astype(jnp.float32)
    estimate = model_init
    low_model = model_init.astype(jnp.bfloat16)
    for iteration in range(ITERS):
        predicted = forward(low_model, left_bases, right_bases, rank_keep)
        residual = apply_gate(predicted - observed, gate_start, gate_stop)
        grad_local = adjoint(residual, left_bases, right_bases, rank_keep)
        gradient = lax.psum(grad_local.astype(jnp.bfloat16), "row").astype(jnp.float32)
        estimate = estimate - step_length * gradient
        low_model = estimate.astype(jnp.bfloat16)
    predicted = forward(low_model, left_bases, right_bases, rank_keep)
    residual = apply_gate(predicted - observed, gate_start, gate_stop)
    return (estimate, residual)


def solution(mesh):
    placed = (
        P(None, None, None, "col"),
        P(None, None, None, ("row", "col")),
        P(("row", "col"), None, None, None, None, None),
        P("row", "col", None, None, None, None),
        P("row", "col", None),
        P(None, ("row", "col")),
        P(None, ("row", "col")),
    )
    return jax.shard_map(
        shards,
        mesh=mesh,
        in_specs=placed,
        out_specs=(P(None, None, None, "col"), P(None, None, None, ("row", "col"))),
        check_vma=False,
    )
```

profile of v0, /device:TPU:0, one launch (start us, length us, event | category | flops | bytes accessed | tf_op | source)
XLA Modules:
  0.0 332.7 jit_solution(16784469923808730853)
XLA Ops:
  7.2 0.8 fusion.96
  8.0 1.0 convert_element_type.93
  9.1 9.1 %fusion.24 = bf16[16,4,2,2,16,96]{5,4,0,3,2,1:T(8,128)(2,1)S(1)} fusion(bf16[16,4,2,96,2,256,1]{5,4,3,2,1,0,6:T(2,128)(2,1)} %bitcast.384, f32[16,4,2,96]{3,0,2,1:T(8,128)S(1)} %get-tuple-element.31, bf16[2,1,16,4,2,256]{5,2,4,1,0,3:T(8,128)(2,1)S(1)} %get-tuple-element.19, bf16[2,1,16,4,2,256]{5,2,4,1,0,3:T(8,128)(2,1)S(1)} %get-tuple-element.18), kind=kOutput, calls=%fused_computation.33 | convolution fusion | flops 403963904 | bytes 13680640 | tf_op jit(solution)/shard_map/jfavcs,ijfkcs->ijfavk/dot_general | solution.py:58
  18.2 1.2 reshape.437
  19.4 1.7 copy.96
  21.1 8.5 %all-to-all-start = ((bf16[16,4,2,2,1536]{4,3,2,1,0:T(2,128)(2,1)}), bf16[16,4,2,2,1536]{4,3,2,1,0:T(2,128)(2,1)S(1)}, u32[]{:S(2)}, u32[]{:S(2)}) async-start(bf16[16,4,2,2,1536]{4,3,2,1,0:T(2,128)(2,1)} %copy.96), calls=%async_computation | async-start | bytes 1572864 | tf_op jit(solution)/shard_map/all_to_all | solution.py:63
  29.8 14.3 %all-to-all-done = bf16[16,4,2,2,1536]{4,3,2,1,0:T(2,128)(2,1)S(1)} async-done(((bf16[16,4,2,2,1536]{4,3,2,1,0:T(2,128)(2,1)}), bf16[16,4,2,2,1536]{4,3,2,1,0:T(2,128)(2,1)S(1)}, u32[]{:S(2)}, u32[]{:S(2)}) %all-to-all-start) | async-done | bytes 786464 | tf_op jit(solution)/shard_map/all_to_all | solution.py:63
  44.4 0.9 reshape.457
  45.4 6.9 %fusion.47 = f32[1,2,2,16,2,256]{5,3,4,2,1,0:T(8,128)S(1)} fusion(bf16[64,2,96,2,256,1]{4,3,2,1,0,5:T(2,128)(2,1)} %bitcast.353, bf16[64,2,2,16,96,1]{4,3,0,2,1,5:T(8,128)(2,1)S(1)} %reshape.457), kind=kOutput, calls=%fused_computation.40 | convolution fusion | flops 402653184 | bytes 13500416 | tf_op jit(solution)/shard_map/ijfavk,ijfkcn->ifavcn/dot_general | solution.py:65
  52.3 1.2 convolution_select_fusion.2
  53.6 0.6 fusion.20
  54.3 7.6 %fusion.35 = bf16[1,64,2,2,16,96]{5,4,1,3,2,0:T(8,128)(2,1)S(1)} fusion(bf16[64,2,96,2,256,1]{4,3,2,1,0,5:T(2,128)(2,1)} %bitcast.354, bf16[2,1,16,1,2,256]{5,2,4,1,0,3:T(8,128)(2,1)S(1)} %get-tuple-element.29, bf16[2,1,16,1,2,256]{5,2,4,1,0,3:T(8,128)(2,1)S(1)} %get-tuple-element.28), kind=kOutput, calls=%fused_computation.36 | convolution fusion | flops 403177472 | bytes 13434880 | tf_op jit(solution)/shard_map/ifavcn,ijfkcn->ijfavk/dot_general | solution.py:74
  61.9 1.2 reshape.442
  63.1 1.7 copy.106
  64.8 3.6 %all-to-all-start.1 = ((bf16[1,64,2,2,1536]{4,3,2,0,1:T(2,128)(2,1)}), bf16[1,64,2,2,1536]{4,3,2,0,1:T(2,128)(2,1)S(1)}, u32[]{:S(2)}, u32[]{:S(2)}) async-start(bf16[1,64,2,2,1536]{4,3,2,0,1:T(2,128)(2,1)} %copy.106), calls=%async_computation.1 | async-start | bytes 1572864 | tf_op jit(solution)/shard_map/all_to_all | solution.py:79
  68.4 0.6 all-reduce.3.cloned.1.call-start
  69.1 12.5 %all-to-all-done.1 = bf16[1,64,2,2,1536]{4,3,2,0,1:T(2,128)(2,1)S(1)} async-done(((bf16[1,64,2,2,1536]{4,3,2,0,1:T(2,128)(2,1)}), bf16[1,64,2,2,1536]{4,3,2,0,1:T(2,128)(2,1)S(1)}, u32[]{:S(2)}, u32[]{:S(2)}) %all-to-all-start.1) | async-done | bytes 786464 | tf_op jit(solution)/shard_map/all_to_all | solution.py:79
  81.7 0.9 reshape.443
  82.6 6.9 %fusion.41 = f32[4,2,2,16,2,256]{5,3,4,2,1,0:T(8,128)S(1)} fusion(bf16[16,4,2,96,2,256,1]{5,4,3,2,1,0,6:T(2,128)(2,1)} %bitcast.385, bf16[16,4,2,2,16,96]{5,4,1,0,3,2:T(8,128)(2,1)S(1)} %reshape.443, bf16[16,4,2,96]{3,1,0,2:T(4,128)(2,1)S(1)} %copy.108), kind=kOutput, calls=%fused_computation.38 | convolution fusion | flops 403046400 | bytes 13918208 | tf_op jit(solution)/shard_map/ijfavk,ijfkcs->jfavcs/dot_general | solution.py:82
  89.6 0.7 copy.210
  90.3 57.5 %all-reduce.3.cloned.1.call-done = bf16[2,2,16,1024]{3,2,1,0:T(8,128)(2,1)} async-done(((bf16[2,2,16,1024]{3,2,1,0:T(8,128)(2,1)}), bf16[2,2,16,1024]{3,2,1,0:T(8,128)(2,1)}) %all-reduce.3.cloned.1.call-update) | async-done | bytes 131088 | tf_op jit(solution)/shard_map/psum | solution.py:97
  147.9 0.9 fusion.68
  149.0 9.1 %fusion.23 = bf16[16,4,2,2,16,96]{5,4,0,3,2,1:T(8,128)(2,1)S(1)} fusion(bf16[16,4,2,96,2,256,1]{5,4,3,2,1,0,6:T(2,128)(2,1)} %bitcast.386, f32[16,4,2,96]{3,0,2,1:T(8,128)S(1)} %get-tuple-element.31, bf16[2,1,16,4,2,256]{5,2,4,1,0,3:T(8,128)(2,1)S(1)} %get-tuple-element.15, bf16[2,1,16,4,2,256]{5,2,4,1,0,3:T(8,128)(2,1)S(1)} %get-tuple-element.14), kind=kOutput, calls=%fused_computation.31 | convolution fusion | flops 403963904 | bytes 13680640 | tf_op jit(solution)/shard_map/jfavcs,ijfkcs->ijfavk/dot_general | solution.py:58
  158.1 1.2 reshape.444
  159.3 0.8 copy.119
  160.1 19.1 %all_to_all.20 = bf16[16,4,2,2,1536]{4,3,2,1,0:T(2,128)(2,1)S(1)} all-to-all(bf16[16,4,2,2,1536]{4,3,2,1,0:T(2,128)(2,1)S(1)} %copy.119), channel_id=1, replica_groups=mesh['row'=8,'col'=16] {'col'}, dimensions={0} | all-to-all | bytes 1572864 | tf_op jit(solution)/shard_map/all_to_all | solution.py:63
  179.5 0.9 reshape.469
  180.4 6.9 %fusion.50 = f32[1,2,2,16,2,256]{5,3,4,2,1,0:T(8,128)S(1)} fusion(bf16[64,2,96,2,256,1]{4,3,2,1,0,5:T(2,128)(2,1)} %bitcast.355, bf16[64,2,2,16,96,1]{4,3,0,2,1,5:T(8,128)(2,1)S(1)} %reshape.469), kind=kOutput, calls=%fused_computation.41 | convolution fusion | flops 402653184 | bytes 13500416 | tf_op jit(solution)/shard_map/ijfavk,ijfkcn->ifavcn/dot_general | solution.py:65
  187.4 1.2 convolution_select_fusion.1
  188.6 0.6 fusion.21
  189.3 7.6 %fusion.38 = bf16[1,64,2,2,16,96]{5,4,1,3,2,0:T(8,128)(2,1)S(1)} fusion(bf16[64,2,96,2,256,1]{4,3,2,1,0,5:T(2,128)(2,1)} %bitcast.356, bf16[2,1,16,1,2,256]{5,2,4,1,0,3:T(8,128)(2,1)S(1)} %get-tuple-element.27, bf16[2,1,16,1,2,256]{5,2,4,1,0,3:T(8,128)(2,1)S(1)} %get-tuple-element.26), kind=kOutput, calls=%fused_computation.37 | convolution fusion | flops 403177472 | bytes 13434880 | tf_op jit(solution)/shard_map/ifavcn,ijfkcn->ijfavk/dot_general | solution.py:74
  197.0 1.2 reshape.448
  198.2 0.8 copy.129
  199.0 14.7 %all_to_all.21 = bf16[1,64,2,2,1536]{4,3,2,0,1:T(2,128)(2,1)S(1)} all-to-all(bf16[1,64,2,2,1536]{4,3,2,0,1:T(2,128)(2,1)S(1)} %copy.129), channel_id=1, replica_groups=mesh['row'=8,'col'=16] {'col'}, dimensions={1} | all-to-all | bytes 1572864 | tf_op jit(solution)/shard_map/all_to_all | solution.py:79
  213.8 0.9 reshape.449
  214.6 6.9 %fusion.44 = f32[4,2,2,16,2,256]{5,3,4,2,1,0:T(8,128)S(1)} fusion(bf16[16,4,2,96,2,256,1]{5,4,3,2,1,0,6:T(2,128)(2,1)} %bitcast.387, bf16[16,4,2,2,16,96]{5,4,1,0,3,2:T(8,128)(2,1)S(1)} %reshape.449, bf16[16,4,2,96]{3,1,0,2:T(4,128)(2,1)S(1)} %copy.108), kind=kOutput, calls=%fused_computation.39 | convolution fusion | flops 403046400 | bytes 13918208 | tf_op jit(solution)/shard_map/ijfavk,ijfkcs->jfavcs/dot_general | solution.py:82
  221.6 0.7 copy.211
  222.3 60.5 %all-reduce.5.cloned.1.call-done = bf16[2,2,16,1024]{3,2,1,0:T(8,128)(2,1)} async-done(((bf16[2,2,16,1024]{3,2,1,0:T(8,128)(2,1)}), bf16[2,2,16,1024]{3,2,1,0:T(8,128)(2,1)}) %all-reduce.5.cloned.1.call-update) | async-done | bytes 131088 | tf_op jit(solution)/shard_map/psum | solution.py:97
  282.8 1.7 fusion.105
  284.6 9.1 %fusion.22 = bf16[16,4,2,2,16,96]{5,4,0,3,2,1:T(8,128)(2,1)S(1)} fusion(bf16[16,4,2,96,2,256,1]{5,4,3,2,1,0,6:T(2,128)(2,1)} %bitcast.388, f32[16,4,2,96]{3,0,2,1:T(8,128)S(1)} %get-tuple-element.31, bf16[2,1,16,4,2,256]{5,2,4,1,0,3:T(8,128)(2,1)S(1)} %get-tuple-element.11, bf16[2,1,16,4,2,256]{5,2,4,1,0,3:T(8,128)(2,1)S(1)} %get-tuple-element.10), kind=kOutput, calls=%fused_computation.29 | convolution fusion | flops 403963904 | bytes 13680640 | tf_op jit(solution)/shard_map/jfavcs,ijfkcs->ijfavk/dot_general | solution.py:58
  293.7 1.2 reshape.450
  294.9 0.8 copy.141
  295.7 19.2 %all_to_all.22 = bf16[16,4,2,2,1536]{4,3,2,1,0:T(2,128)(2,1)S(1)} all-to-all(bf16[16,4,2,2,1536]{4,3,2,1,0:T(2,128)(2,1)S(1)} %copy.141), channel_id=1, replica_groups=mesh['row'=8,'col'=16] {'col'}, dimensions={0} | all-to-all | bytes 1572864 | tf_op jit(solution)/shard_map/all_to_all | solution.py:63
  315.2 0.9 reshape.481
  316.1 6.9 %fusion.53 = f32[1,2,2,16,2,256]{5,3,4,2,1,0:T(8,128)S(1)} fusion(bf16[64,2,96,2,256,1]{4,3,2,1,0,5:T(2,128)(2,1)} %bitcast.357, bf16[64,2,2,16,96,1]{4,3,0,2,1,5:T(8,128)(2,1)S(1)} %reshape.481), kind=kOutput, calls=%fused_computation.42 | convolution fusion | flops 402653184 | bytes 13500416 | tf_op jit(solution)/shard_map/ijfavk,ijfkcn->ifavcn/dot_general | solution.py:65
  323.1 1.2 convolution_select_fusion
  324.3 0.6 convolution_multiply_fusion
  324.9 0.6 copy.221
  (69 shorter events, 2.3 us)
Async XLA Ops:
  7.2 22.4 %copy-start.3 = (s32[16,256]{1,0:T(8,128)S(1)}, s32[16,256]{1,0:T(8,128)}, u32[]{:S(2)}) copy-start(s32[16,256]{1,0:T(8,128)} %param.12) | copy-start | bytes 49156
  7.2 22.5 %copy-start.4 = (s32[16,256]{1,0:T(8,128)S(1)}, s32[16,256]{1,0:T(8,128)}, u32[]{:S(2)}) copy-start(s32[16,256]{1,0:T(8,128)} %param.13) | copy-start | bytes 49156
  18.2 34.1 %copy-start.1 = (f32[2,2,16,256]{3,2,1,0:T(8,128)S(1)}, f32[2,2,16,256]{3,2,1,0:T(8,128)}, u32[]{:S(2)}) copy-start(f32[2,2,16,256]{3,2,1,0:T(8,128)} %param.8) | copy-start | bytes 196612
  21.1 23.0 %all-to-all-start = ((bf16[16,4,2,2,1536]{4,3,2,1,0:T(2,128)(2,1)}), bf16[16,4,2,2,1536]{4,3,2,1,0:T(2,128)(2,1)S(1)}, u32[]{:S(2)}, u32[]{:S(2)}) async-start(bf16[16,4,2,2,1536]{4,3,2,1,0:T(2,128)(2,1)} %copy.96), calls=%async_computation | async-start | bytes 1572864 | tf_op jit(solution)/shard_map/all_to_all | solution.py:63
  61.9 86.0 %copy-start = (f32[2,2,16,1024]{3,2,1,0:T(8,128)S(1)}, f32[2,2,16,1024]{3,2,1,0:T(8,128)}, u32[]{:S(2)}) copy-start(f32[2,2,16,1024]{3,2,1,0:T(8,128)} %param.7) | copy-start | bytes 786436
  64.8 16.8 %all-to-all-start.1 = ((bf16[1,64,2,2,1536]{4,3,2,0,1:T(2,128)(2,1)}), bf16[1,64,2,2,1536]{4,3,2,0,1:T(2,128)(2,1)S(1)}, u32[]{:S(2)}, u32[]{:S(2)}) async-start(bf16[1,64,2,2,1536]{4,3,2,0,1:T(2,128)(2,1)} %copy.106), calls=%async_computation.1 | async-start | bytes 1572864 | tf_op jit(solution)/shard_map/all_to_all | solution.py:79
  68.4 79.4 %all-reduce.3.cloned.1.call-start = ((), (), s32[]{:S(2)}) async-start(), calls=%async_computation.5 | async-start | bytes 262144 | tf_op jit(solution)/shard_map/psum | solution.py:97
  90.3 192.5 %all-reduce.5.cloned.1.call-start = ((), (), s32[]{:S(2)}) async-start(), calls=%async_computation.6 | async-start | bytes 262144 | tf_op jit(solution)/shard_map/psum | solution.py:97
  196.9 85.8 %copy-start.2 = (bf16[2,2,16,1024]{3,2,1,0:T(8,128)(2,1)S(1)}, bf16[2,2,16,1024]{3,2,1,0:T(8,128)(2,1)}, u32[]{:S(2)}) copy-start(bf16[2,2,16,1024]{3,2,1,0:T(8,128)(2,1)} %all-reduce.3.cloned.1.call-done) | copy-start | bytes 393220
Sparse Core Ops, SparseCore 0:
  90.4 57.4 all-reduce.2
  222.4 60.2 all-reduce.4
where the time goes:
time: 338 us; the launch traced here: 333 us
  waiting for transfers between devices  145 us (43%)
  matrix products  82.3 us (24%)
  blocking collectives  52.9 us (16%)
  local copies, waits for them, and re-layouts  20.1 us (6%)
  between operations  14.9 us (4%)
  starting transfers between devices  12.8 us (4%)
  other arithmetic  4.84 us (1%)
    psum x2, waiting for transfers between devices, shards(): lax.psum(grad_local.astype(jnp.bfloat16), 'row').astype(jnp.float32)  118 us
    all_to_all x2, blocking collectives, forward(): lax.all_to_all(sendable, 'col', split_axis=0, concat_axis=1, tiled=True)  38.2 us
    dot_general x3, matrix products, forward(): jnp.einsum('jfavcs,ijfkcs->ijfavk', paired, right_bases, preferred_elemen...  27.3 us
    dot_general x3, matrix products, forward(): jnp.einsum('ijfavk,ijfkcn->ifavcn', received, left_bases, preferred_eleme...  20.6 us
    dot_general x2, matrix products, adjoint(): jnp.einsum('ifavcn,ijfkcn->ijfavk', paired, left_bases, preferred_element...  15.2 us
    all_to_all x1, blocking collectives, adjoint(): lax.all_to_all(sendable, 'col', split_axis=1, concat_axis=0, tiled=True)  14.7 us
    all_to_all x1, waiting for transfers between devices, forward(): lax.all_to_all(sendable, 'col', split_axis=0, concat_axis=1, tiled=True)  14.3 us
    dot_general x2, matrix products, adjoint(): jnp.einsum('ijfavk,ijfkcs->jfavcs', received, right_bases, preferred_elem...  13.8 us
  transfers between devices with their start and end apart: 4, of which 4 were waited for; matrix products, arithmetic and copies ran while one was open for 0% of the time, Pallas kernels for 0%

commit v1 on v0

v1 whole, which is shorter than its diff:
```python
import math

import jax
import jax.numpy as jnp
from jax import lax
from jax.experimental import pallas as pl
from jax.experimental.pallas import tpu as pltpu
from jax.sharding import PartitionSpec as P

NV = 16
TILE = 256
RMAX = 96
F = 2
NT = 64
ITERS = 2
WIDE = F * RMAX * 2
ROWS = F * 2 * NV

step_length = 0.8


def lane_facts(rows):
    lane = lax.broadcasted_iota(jnp.int32, (rows, WIDE), 1)
    return lane % 2 == 0, lane < WIDE // 2, lane


def project(field, basis, even, first):
    z = lax.dot_general(field, basis, (((1,), (1,)), ((), ())), preferred_element_type=jnp.float32)
    real = jnp.where(first, z[0:NV], z[2 * NV : 3 * NV])
    imag = jnp.where(first, z[NV : 2 * NV], z[3 * NV :])
    ahead = pltpu.roll(imag, WIDE - 1, 1)
    behind = pltpu.roll(imag, 1, 1)
    return real + jnp.where(even, ahead, -behind)


def expand(packed, basis, even, first):
    wide = packed.astype(jnp.float32)
    ahead = pltpu.roll(wide, WIDE - 1, 1)
    behind = pltpu.roll(wide, 1, 1)
    swapped = jnp.where(even, -ahead, behind)
    zero = jnp.zeros_like(wide)
    left = jnp.concatenate(
        [
            jnp.where(first, wide, zero),
            jnp.where(first, swapped, zero),
            jnp.where(first, zero, wide),
            jnp.where(first, zero, swapped),
        ],
        axis=0,
    ).astype(jnp.bfloat16)
    return jnp.dot(left, basis, preferred_element_type=jnp.float32)


def forward_kernel(model_ref, basis_ref, ranks_ref, out_ref):
    even, first, lane = lane_facts(NV)
    rank_of_lane = jnp.where(first, lane, lane - WIDE // 2) // 2
    for j in range(4):
        field = jnp.concatenate(
            [model_ref[a, f, :, j * TILE : (j + 1) * TILE] for f in range(F) for a in range(2)], axis=0
        ).astype(jnp.bfloat16)

        def one(i, carry):
            tile = i * 4 + j
            x = project(field, basis_ref[tile], even, first)
            limit = jnp.where(first, ranks_ref[tile, 0], ranks_ref[tile, 1])
            x = jnp.where(rank_of_lane < limit, x, 0.0)
            out_ref[tile] = x.astype(jnp.bfloat16)
            return carry

        lax.fori_loop(0, 16, one, 0, unroll=4)


def gate(re0, im0, re1, im1, start, stop):
    outs = [jnp.zeros_like(re0) for _ in range(4)]
    for t in range(NT):
        rows = []
        for f in range(F):
            phase = 2.0 * math.pi * ((3 + 5 * f) * t % NT) / NT
            rows += [math.cos(phase), -math.sin(phase)]
        signal = re0 * rows[0] + im0 * rows[1] + re1 * rows[2] + im1 * rows[3]
        signal = jnp.where((start <= t) & (stop > t), signal, 0.0)
        outs = [o + signal * r for o, r in zip(outs, rows)]
    return [o * (2.0 / NT) for o in outs]


def residual_parts(got_ref, basis_ref, observed_ref, start_ref, stop_ref, total_ref):
    even, first, _ = lane_facts(NV)
    total_ref[...] = jnp.zeros_like(total_ref)

    def one(j, carry):
        total_ref[...] += expand(got_ref[j], basis_ref[j], even, first)
        return carry

    lax.fori_loop(0, 64, one, 0, unroll=4)
    parts = [
        total_ref[(2 * f + a) * NV : (2 * f + a + 1) * NV] - observed_ref[a, f] for f in range(F) for a in range(2)
    ]
    return gate(*parts, start_ref[...], stop_ref[...])


def middle_kernel(got_ref, basis_ref, observed_ref, start_ref, stop_ref, out_ref, total_ref):
    parts = residual_parts(got_ref, basis_ref, observed_ref, start_ref, stop_ref, total_ref)
    field = jnp.concatenate(parts, axis=0).astype(jnp.bfloat16)
    even, first, _ = lane_facts(NV)

    def one(j, carry):
        out_ref[j] = project(field, basis_ref[j], even, first).astype(jnp.bfloat16)
        return carry

    lax.fori_loop(0, 64, one, 0, unroll=4)


def last_kernel(got_ref, basis_ref, observed_ref, start_ref, stop_ref, out_ref, total_ref):
    parts = residual_parts(got_ref, basis_ref, observed_ref, start_ref, stop_ref, total_ref)
    for f in range(F):
        for a in range(2):
            out_ref[a, f] = parts[2 * f + a]


def gradient_kernel(got_ref, basis_ref, ranks_ref, out_ref, total_ref):
    even, first, lane = lane_facts(NV)
    rank_of_lane = jnp.where(first, lane, lane - WIDE // 2) // 2
    for j in range(4):
        total_ref[...] = jnp.zeros_like(total_ref)

        def one(i, carry):
            tile = i * 4 + j
            limit = jnp.where(first, ranks_ref[tile, 0], ranks_ref[tile, 1])
            kept = jnp.where(rank_of_lane < limit, got_ref[tile].astype(jnp.float32), 0.0)
            total_ref[...] += expand(kept, basis_ref[tile], even, first)
            return carry

        lax.fori_loop(0, 16, one, 0, unroll=4)
        for f in range(F):
            for a in range(2):
                row = (2 * f + a) * NV
                out_ref[a, f, :, j * TILE : (j + 1) * TILE] = total_ref[row : row + NV]


VMEM = pl.BlockSpec(memory_space=pltpu.VMEM)
SMEM = pl.BlockSpec(memory_space=pltpu.SMEM)
PACKED = jax.ShapeDtypeStruct((64, NV, WIDE), jnp.bfloat16)
TOTAL = pltpu.VMEM((ROWS, TILE), jnp.float32)
PARAMS = pltpu.CompilerParams(vmem_limit_bytes=40 * 1024 * 1024)


def call(kernel, specs, out, scratch):
    return pl.pallas_call(
        kernel,
        out_shape=out,
        in_specs=specs,
        out_specs=VMEM,
        scratch_shapes=scratch,
        compiler_params=PARAMS,
        name=kernel.__name__,
    )


def exchange(packed):
    parts = packed.reshape(16, 4, NV, WIDE)
    return lax.all_to_all(parts, "col", 0, 0, tiled=True).reshape(64, NV, WIDE)


def row_sum(local):
    low = local.astype(jnp.bfloat16).astype(jnp.float32)
    for step in (1, 2, 4):
        other = lax.ppermute(low.astype(jnp.bfloat16), "row", [(d, d ^ step) for d in range(8)])
        low = low.astype(jnp.bfloat16).astype(jnp.float32) + other.astype(jnp.float32)
    return low


def shards(model_init, observed, left_bases, right_bases, tile_ranks, gate_start, gate_stop):
    left = left_bases.reshape(64, WIDE, TILE)
    right = right_bases.reshape(64, WIDE, TILE)
    ranks = tile_ranks.reshape(64, F)
    forward = call(forward_kernel, [VMEM, VMEM, SMEM], PACKED, [])
    middle = call(middle_kernel, [VMEM] * 5, PACKED, [TOTAL])
    last = call(last_kernel, [VMEM] * 5, jax.ShapeDtypeStruct((2, F, NV, TILE), jnp.float32), [TOTAL])
    gradient = call(
        gradient_kernel, [VMEM, VMEM, SMEM], jax.ShapeDtypeStruct((2, F, NV, 1024), jnp.float32), [TOTAL]
    )
    estimate = model_init
    for iteration in range(ITERS):
        got = exchange(forward(estimate, right, ranks))
        back = exchange(middle(got, left, observed, gate_start, gate_stop))
        estimate = estimate - step_length * row_sum(gradient(back, right, ranks))
    got = exchange(forward(estimate, right, ranks))
    return estimate, last(got, left, observed, gate_start, gate_stop)


def solution(mesh):
    placed = (
        P(None, None, None, "col"),
        P(None, None, None, ("row", "col")),
        P(("row", "col"), None, None, None, None, None),
        P("row", "col", None, None, None, None),
        P("row", "col", None),
        P(None, ("row", "col")),
        P(None, ("row", "col")),
    )
    return jax.shard_map(
        shards,
        mesh=mesh,
        in_specs=placed,
        out_specs=(P(None, None, None, "col"), P(None, None, None, ("row", "col"))),
        check_vma=False,
    )
```

time: 338 us -> 240 us (0.71)
  waiting for transfers between devices: 145 us -> 17.7 us
  matrix products: 82.3 us -> 0 us
  Pallas kernels: 0 us -> 68.3 us
  local copies, waits for them, and re-layouts: 20.1 us -> 66.4 us
  between operations: 14.9 us -> 0.8 us
  blocking collectives: 52.9 us -> 66.9 us
  starting transfers between devices: 12.8 us -> 17.7 us
  other arithmetic: 4.84 us -> 0.25 us
    psum x2 -> x0, waiting for transfers between devices: 118 us -> none  [shards(): lax.psum(grad_local.astype(jnp.bfloat16), 'row').astype(jnp.float32)]
    dot_general x16 -> x0, matrix products: 82.3 us -> none  [the longest x3 27.3 us: forward(): jnp.einsum('jfavcs,ijfkcs->ijfavk', paired, right_bases, preferred_elemen...]
    pallas_call x0 -> x8, Pallas kernels: none -> 68.3 us  [the longest x2 25 us: shards(): back = exchange(middle(got, left, observed, gate_start, gate_stop))]
    all_to_all x2 -> x1, waiting for transfers between devices: 26.8 us -> 0.01 us  [exchange(): return lax.all_to_all(parts, 'col', 0, 0, tiled=True).reshape(64, NV, WIDE)]
    unnamed x18 -> x22, local copies, waits for them, and re-layouts: 0.84 us -> 27.5 us
    reshape x12 -> x3, local copies, waits for them, and re-layouts: 13.6 us -> 38.9 us  [the longest x1 19.1 us: shards(): left = left_bases.reshape(64, WIDE, TILE)]
    ppermute x0 -> x6, waiting for transfers between devices: none -> 17.7 us  [row_sum(): lax.ppermute(low.astype(jnp.bfloat16), 'row', [(d, d ^ step) for d in ran...]
    all_to_all x3 -> x4, blocking collectives: 52.9 us -> 66.9 us  [exchange(): return lax.all_to_all(parts, 'col', 0, 0, tiled=True).reshape(64, NV, WIDE)]
  transfers between devices with their start and end apart: 4 -> 7, of which waited for: 4 -> 6; matrix products, arithmetic and copies ran while one was open for 0% -> 8% of each run, Pallas kernels for 0% -> 0%
where the time goes in v1:
time: 240 us; the launch traced here: 238 us
  Pallas kernels  68.3 us (28%)
  blocking collectives  66.9 us (28%)
  local copies, waits for them, and re-layouts  66.4 us (28%)
  starting transfers between devices  17.7 us (7%)
  waiting for transfers between devices  17.7 us (7%)
    all_to_all x4, blocking collectives, exchange(): return lax.all_to_all(parts, 'col', 0, 0, tiled=True).reshape(64, NV, WIDE)  66.9 us
    unnamed x22, local copies, waits for them, and re-layouts  27.5 us
    pallas_call x2, Pallas kernels, shards(): back = exchange(middle(got, left, observed, gate_start, gate_stop))  25 us
    pallas_call x3, Pallas kernels, shards(): got = exchange(forward(estimate, right, ranks))  24.8 us
    reshape x1, local copies, waits for them, and re-layouts, shards(): left = left_bases.reshape(64, WIDE, TILE)  19.1 us
    reshape x1, local copies, waits for them, and re-layouts, shards(): right = right_bases.reshape(64, WIDE, TILE)  19.1 us
    ppermute x6, waiting for transfers between devices, row_sum(): lax.ppermute(low.astype(jnp.bfloat16), 'row', [(d, d ^ step) for d in ran...  17.7 us
    pallas_call x2, Pallas kernels, shards(): estimate = estimate - step_length * row_sum(gradient(back, right, ranks))  12.3 us
  transfers between devices with their start and end apart: 7, of which 6 were waited for; matrix products, arithmetic and copies ran while one was open for 8% of the time, Pallas kernels for 0%

profile of v1, /device:TPU:0, one launch (start us, length us, event | category | flops | bytes accessed | tf_op | source)
XLA Modules:
  0.0 238.0 jit_solution(15063981321589311396)
XLA Ops:
  0.6 0.8 copy.21
  1.4 0.0 copy-start.6
  1.4 19.1 %reshape.43.basis_ref = bf16[64,384,256]{2,1,0:T(8,128)(2,1)} reshape(bf16[16,4,2,96,2,256]{5,4,3,2,1,0:T(2,128)(2,1)} %param.10) | data formatting | bytes 25165824 | tf_op jit(solution)/shard_map/reshape | solution.py:174
  20.5 0.0 copy-done.6
  20.5 0.0 copy-start
  20.5 4.6 %copy-done = bf16[64,384,256]{2,1,0:T(8,128)(2,1)S(1)} copy-done((bf16[64,384,256]{2,1,0:T(8,128)(2,1)S(1)}, bf16[64,384,256]{2,1,0:T(8,128)(2,1)}, u32[]{:S(2)}) %copy-start) | copy-done | bytes 12582936
  25.1 8.9 %forward_kernel.3 = bf16[64,16,384]{2,1,0:T(8,128)(2,1)} custom-call(f32[2,2,16,1024]{3,2,1,0:T(8,128)S(1)} %copy-done.6, bf16[64,384,256]{2,1,0:T(8,128)(2,1)S(1)} %copy-done, s32[64,2]{1,0:T(8,128)S(1)} %bitcast.20), custom_call_target="tpu_custom_call" | custom-call | tf_op jit(solution)/shard_map/forward_kernel/pallas_call | solution.py:184
  34.0 8.2 %all-to-all-start = ((bf16[16,4,16,384]{3,2,1,0:T(8,128)(2,1)}), bf16[16,4,16,384]{3,2,1,0:T(8,128)(2,1)S(1)}, u32[]{:S(2)}, u32[]{:S(2)}) async-start(bf16[16,4,16,384]{3,2,1,0:T(8,128)(2,1)} %bitcast.1), calls=%async_computation | async-start | bytes 1572864 | tf_op jit(solution)/shard_map/all_to_all | solution.py:161
  42.1 0.0 copy-start.8
  42.2 0.0 copy-start.9
  42.2 0.0 copy-start.10
  42.2 19.1 %reshape.47.basis_ref = bf16[64,384,256]{2,1,0:T(8,128)(2,1)} reshape(bf16[1,64,2,96,2,256]{5,4,3,2,1,0:T(2,128)(2,1)} %param.9) | data formatting | bytes 25165824 | tf_op jit(solution)/shard_map/reshape | solution.py:173
  61.2 0.0 all-to-all-done
  61.2 0.0 copy-done.8
  61.2 0.0 copy-done.9
  61.2 0.0 copy-done.10
  61.3 0.0 copy-start.3
  61.3 4.6 %copy-done.3 = bf16[64,384,256]{2,1,0:T(8,128)(2,1)S(1)} copy-done((bf16[64,384,256]{2,1,0:T(8,128)(2,1)S(1)}, bf16[64,384,256]{2,1,0:T(8,128)(2,1)}, u32[]{:S(2)}) %copy-start.3) | copy-done | bytes 12582936
  65.8 12.5 %middle_kernel.2 = bf16[64,16,384]{2,1,0:T(8,128)(2,1)S(1)} custom-call(bf16[64,16,384]{2,1,0:T(8,128)(2,1)S(1)} %bitcast.11, bf16[64,384,256]{2,1,0:T(8,128)(2,1)S(1)} %copy-done.3, f32[2,2,16,256]{3,2,1,0:T(8,128)S(1)} %copy-done.8, s32[16,256]{1,0:T(8,128)S(1)} %copy-done.9, s32[16,256]{1,0:T(8,128)S(1)} %copy-done.10), custom_call_target="tpu_custom_call" | custom-call | tf_op jit(solution)/shard_map/middle_kernel/pallas_call | solution.py:185
  78.3 20.8 %all_to_all.25 = bf16[16,4,16,384]{3,2,1,0:T(8,128)(2,1)S(1)} all-to-all(bf16[16,4,16,384]{3,2,1,0:T(8,128)(2,1)S(1)} %bitcast.13), channel_id=1, replica_groups=mesh['row'=8,'col'=16] {'col'}, dimensions={0} | all-to-all | bytes 1572864 | tf_op jit(solution)/shard_map/all_to_all | solution.py:161
  99.1 0.0 copy-start.1
  99.1 4.6 %copy-done.1 = bf16[64,384,256]{2,1,0:T(8,128)(2,1)S(1)} copy-done((bf16[64,384,256]{2,1,0:T(8,128)(2,1)S(1)}, bf16[64,384,256]{2,1,0:T(8,128)(2,1)}, u32[]{:S(2)}) %copy-start.1) | copy-done | bytes 12582936
  103.7 6.2 %gradient_kernel.2 = f32[2,2,16,1024]{3,2,1,0:T(8,128)S(1)} custom-call(bf16[64,16,384]{2,1,0:T(8,128)(2,1)S(1)} %bitcast.17, bf16[64,384,256]{2,1,0:T(8,128)(2,1)S(1)} %copy-done.1, s32[64,2]{1,0:T(8,128)S(1)} %bitcast.21), custom_call_target="tpu_custom_call" | custom-call | tf_op jit(solution)/shard_map/gradient_kernel/pallas_call | solution.py:186
  109.9 0.1 collective-permute-start
  110.0 1.3 collective-permute-done
  111.3 1.6 collective-permute-start.1
  112.9 4.1 %collective-permute-done.1 = bf16[2,2,16,1024]{3,2,1,0:T(8,128)(2,1)S(1)} collective-permute-done((bf16[2,2,16,1024]{3,2,1,0:T(8,128)(2,1)S(1)}, bf16[2,2,16,1024]{3,2,1,0:T(8,128)(2,1)S(1)}, u32[]{:S(2)}, u32[]{:S(2)}) %collective-permute-start.1) | collective-permute-done | bytes 131104 | tf_op jit(solution)/shard_map/ppermute | solution.py:167
  117.0 3.1 %collective-permute-start.2 = (bf16[2,2,16,1024]{3,2,1,0:T(8,128)(2,1)S(1)}, bf16[2,2,16,1024]{3,2,1,0:T(8,128)(2,1)S(1)}, u32[]{:S(2)}, u32[]{:S(2)}) collective-permute-start(bf16[2,2,16,1024]{3,2,1,0:T(8,128)(2,1)S(1)} %add_convert_fusion.2), channel_id=1, source_target_pairs={{0,64},{16,80},{32,96},{48,112},{64,0},{80,16},{96,32},{112,48},{1... | collective-permute-start | bytes 393224 | tf_op jit(solution)/shard_map/ppermute | solution.py:167
  120.1 3.5 %collective-permute-done.2 = bf16[2,2,16,1024]{3,2,1,0:T(8,128)(2,1)S(1)} collective-permute-done((bf16[2,2,16,1024]{3,2,1,0:T(8,128)(2,1)S(1)}, bf16[2,2,16,1024]{3,2,1,0:T(8,128)(2,1)S(1)}, u32[]{:S(2)}, u32[]{:S(2)}) %collective-permute-start.2) | collective-permute-done | bytes 131104 | tf_op jit(solution)/shard_map/ppermute | solution.py:167
  123.6 7.9 %forward_kernel.4 = bf16[64,16,384]{2,1,0:T(8,128)(2,1)S(1)} custom-call(f32[2,2,16,1024]{3,2,1,0:T(8,128)S(1)} %multiply_subtract_fusion.1.model_ref, bf16[64,384,256]{2,1,0:T(8,128)(2,1)S(1)} %copy-done.1, s32[64,2]{1,0:T(8,128)S(1)} %bitcast.22), custom_call_target="tpu_custom_call" | custom-call | tf_op jit(solution)/shard_map/forward_kernel/pallas_call | solution.py:184
  131.6 15.6 %all_to_all.26 = bf16[16,4,16,384]{3,2,1,0:T(8,128)(2,1)S(1)} all-to-all(bf16[16,4,16,384]{3,2,1,0:T(8,128)(2,1)S(1)} %bitcast.19), channel_id=1, replica_groups=mesh['row'=8,'col'=16] {'col'}, dimensions={0} | all-to-all | bytes 1572864 | tf_op jit(solution)/shard_map/all_to_all | solution.py:161
  147.2 4.6 %copy-done.4 = bf16[64,384,256]{2,1,0:T(8,128)(2,1)S(1)} copy-done((bf16[64,384,256]{2,1,0:T(8,128)(2,1)S(1)}, bf16[64,384,256]{2,1,0:T(8,128)(2,1)}, u32[]{:S(2)}) %copy-start.4) | copy-done | bytes 12582936
  151.8 12.5 %middle_kernel.3 = bf16[64,16,384]{2,1,0:T(8,128)(2,1)S(1)} custom-call(bf16[64,16,384]{2,1,0:T(8,128)(2,1)S(1)} %bitcast.14, bf16[64,384,256]{2,1,0:T(8,128)(2,1)S(1)} %copy-done.4, f32[2,2,16,256]{3,2,1,0:T(8,128)S(1)} %copy-done.8, s32[16,256]{1,0:T(8,128)S(1)} %copy-done.9, s32[16,256]{1,0:T(8,128)S(1)} %copy-done.10), custom_call_target="tpu_custom_call" | custom-call | tf_op jit(solution)/shard_map/middle_kernel/pallas_call | solution.py:185
  164.3 14.9 %all_to_all.27 = bf16[16,4,16,384]{3,2,1,0:T(8,128)(2,1)S(1)} all-to-all(bf16[16,4,16,384]{3,2,1,0:T(8,128)(2,1)S(1)} %bitcast.15), channel_id=1, replica_groups=mesh['row'=8,'col'=16] {'col'}, dimensions={0} | all-to-all | bytes 1572864 | tf_op jit(solution)/shard_map/all_to_all | solution.py:161
  179.2 4.6 %copy-done.2 = bf16[64,384,256]{2,1,0:T(8,128)(2,1)S(1)} copy-done((bf16[64,384,256]{2,1,0:T(8,128)(2,1)S(1)}, bf16[64,384,256]{2,1,0:T(8,128)(2,1)}, u32[]{:S(2)}) %copy-start.2) | copy-done | bytes 12582936
  183.8 6.2 %gradient_kernel.3 = f32[2,2,16,1024]{3,2,1,0:T(8,128)S(1)} custom-call(bf16[64,16,384]{2,1,0:T(8,128)(2,1)S(1)} %bitcast.18, bf16[64,384,256]{2,1,0:T(8,128)(2,1)S(1)} %copy-done.2, s32[64,2]{1,0:T(8,128)S(1)} %bitcast.23), custom_call_target="tpu_custom_call" | custom-call | tf_op jit(solution)/shard_map/gradient_kernel/pallas_call | solution.py:186
  189.9 0.1 collective-permute-start.3
  190.0 1.3 collective-permute-done.3
  191.4 1.6 collective-permute-start.4
  193.0 4.1 %collective-permute-done.4 = bf16[2,2,16,1024]{3,2,1,0:T(8,128)(2,1)S(1)} collective-permute-done((bf16[2,2,16,1024]{3,2,1,0:T(8,128)(2,1)S(1)}, bf16[2,2,16,1024]{3,2,1,0:T(8,128)(2,1)S(1)}, u32[]{:S(2)}, u32[]{:S(2)}) %collective-permute-start.4) | collective-permute-done | bytes 131104 | tf_op jit(solution)/shard_map/ppermute | solution.py:167
  197.1 3.1 %collective-permute-start.5 = (bf16[2,2,16,1024]{3,2,1,0:T(8,128)(2,1)S(1)}, bf16[2,2,16,1024]{3,2,1,0:T(8,128)(2,1)S(1)}, u32[]{:S(2)}, u32[]{:S(2)}) collective-permute-start(bf16[2,2,16,1024]{3,2,1,0:T(8,128)(2,1)S(1)} %add_convert_fusion), channel_id=1, source_target_pairs={{0,64},{16,80},{32,96},{48,112},{64,0},{80,16},{96,32},{112,48},{1... | collective-permute-start | bytes 393224 | tf_op jit(solution)/shard_map/ppermute | solution.py:167
  200.2 3.5 %collective-permute-done.5 = bf16[2,2,16,1024]{3,2,1,0:T(8,128)(2,1)S(1)} collective-permute-done((bf16[2,2,16,1024]{3,2,1,0:T(8,128)(2,1)S(1)}, bf16[2,2,16,1024]{3,2,1,0:T(8,128)(2,1)S(1)}, u32[]{:S(2)}, u32[]{:S(2)}) %collective-permute-start.5) | collective-permute-done | bytes 131104 | tf_op jit(solution)/shard_map/ppermute | solution.py:167
  203.7 0.0 copy-start.7
  203.7 7.9 %forward_kernel.5 = bf16[64,16,384]{2,1,0:T(8,128)(2,1)S(1)} custom-call(f32[2,2,16,1024]{3,2,1,0:T(8,128)S(1)} %multiply_subtract_fusion.model_ref, bf16[64,384,256]{2,1,0:T(8,128)(2,1)S(1)} %copy-done.2, s32[64,2]{1,0:T(8,128)S(1)} %bitcast.24), custom_call_target="tpu_custom_call" | custom-call | tf_op jit(solution)/shard_map/forward_kernel/pallas_call | solution.py:187
  211.6 15.6 %all_to_all.28 = bf16[16,4,16,384]{3,2,1,0:T(8,128)(2,1)S(1)} all-to-all(bf16[16,4,16,384]{3,2,1,0:T(8,128)(2,1)S(1)} %bitcast.16), channel_id=1, replica_groups=mesh['row'=8,'col'=16] {'col'}, dimensions={0} | all-to-all | bytes 1572864 | tf_op jit(solution)/shard_map/all_to_all | solution.py:161
  227.2 4.6 %copy-done.5 = bf16[64,384,256]{2,1,0:T(8,128)(2,1)S(1)} copy-done((bf16[64,384,256]{2,1,0:T(8,128)(2,1)S(1)}, bf16[64,384,256]{2,1,0:T(8,128)(2,1)}, u32[]{:S(2)}) %copy-start.5) | copy-done | bytes 12582936
  231.8 6.2 %last_kernel.1 = f32[2,2,16,256]{3,2,1,0:T(8,128)} custom-call(bf16[64,16,384]{2,1,0:T(8,128)(2,1)S(1)} %bitcast.12, bf16[64,384,256]{2,1,0:T(8,128)(2,1)S(1)} %copy-done.5, f32[2,2,16,256]{3,2,1,0:T(8,128)S(1)} %copy-done.8, s32[16,256]{1,0:T(8,128)S(1)} %copy-done.9, s32[16,256]{1,0:T(8,128)S(1)} %copy-done.10), custom_call_target="tpu_custom_call" | custom-call | tf_op jit(solution)/shard_map/last_kernel/pallas_call | solution.py:188
  238.0 0.0 copy-done.7
  (11 shorter events, 0.3 us)
Async XLA Ops:
  1.4 19.1 %copy-start.6 = (f32[2,2,16,1024]{3,2,1,0:T(8,128)S(1)}, f32[2,2,16,1024]{3,2,1,0:T(8,128)}, u32[]{:S(2)}) copy-start(f32[2,2,16,1024]{3,2,1,0:T(8,128)} %model_ref.1) | copy-start | bytes 786436
  20.5 4.6 %copy-start = (bf16[64,384,256]{2,1,0:T(8,128)(2,1)S(1)}, bf16[64,384,256]{2,1,0:T(8,128)(2,1)}, u32[]{:S(2)}) copy-start(bf16[64,384,256]{2,1,0:T(8,128)(2,1)} %reshape.43.basis_ref) | copy-start | bytes 37748740
  34.0 27.3 %all-to-all-start = ((bf16[16,4,16,384]{3,2,1,0:T(8,128)(2,1)}), bf16[16,4,16,384]{3,2,1,0:T(8,128)(2,1)S(1)}, u32[]{:S(2)}, u32[]{:S(2)}) async-start(bf16[16,4,16,384]{3,2,1,0:T(8,128)(2,1)} %bitcast.1), calls=%async_computation | async-start | bytes 1572864 | tf_op jit(solution)/shard_map/all_to_all | solution.py:161
  42.1 19.1 %copy-start.8 = (f32[2,2,16,256]{3,2,1,0:T(8,128)S(1)}, f32[2,2,16,256]{3,2,1,0:T(8,128)}, u32[]{:S(2)}) copy-start(f32[2,2,16,256]{3,2,1,0:T(8,128)} %observed_ref.5) | copy-start | bytes 196612
  42.2 19.1 %copy-start.9 = (s32[16,256]{1,0:T(8,128)S(1)}, s32[16,256]{1,0:T(8,128)}, u32[]{:S(2)}) copy-start(s32[16,256]{1,0:T(8,128)} %start_ref.5) | copy-start | bytes 49156
  42.2 19.1 %copy-start.10 = (s32[16,256]{1,0:T(8,128)S(1)}, s32[16,256]{1,0:T(8,128)}, u32[]{:S(2)}) copy-start(s32[16,256]{1,0:T(8,128)} %stop_ref.5) | copy-start | bytes 49156
  61.3 4.6 %copy-start.3 = (bf16[64,384,256]{2,1,0:T(8,128)(2,1)S(1)}, bf16[64,384,256]{2,1,0:T(8,128)(2,1)}, u32[]{:S(2)}) copy-start(bf16[64,384,256]{2,1,0:T(8,128)(2,1)} %reshape.47.basis_ref) | copy-start | bytes 37748740
  99.1 4.6 %copy-start.1 = (bf16[64,384,256]{2,1,0:T(8,128)(2,1)S(1)}, bf16[64,384,256]{2,1,0:T(8,128)(2,1)}, u32[]{:S(2)}) copy-start(bf16[64,384,256]{2,1,0:T(8,128)(2,1)} %reshape.43.basis_ref) | copy-start | bytes 37748740
  109.9 1.4 collective-permute-start
  111.3 5.6 %collective-permute-start.1 = (bf16[2,2,16,1024]{3,2,1,0:T(8,128)(2,1)S(1)}, bf16[2,2,16,1024]{3,2,1,0:T(8,128)(2,1)S(1)}, u32[]{:S(2)}, u32[]{:S(2)}) collective-permute-start(bf16[2,2,16,1024]{3,2,1,0:T(8,128)(2,1)S(1)} %add_convert_fusion.3), channel_id=1, source_target_pairs={{0,32},{16,48},{32,0},{48,16},{64,96},{80,112},{96,64},{112,80},{1... | collective-permute-start | bytes 393224 | tf_op jit(solution)/shard_map/ppermute | solution.py:167
  117.0 6.6 %collective-permute-start.2 = (bf16[2,2,16,1024]{3,2,1,0:T(8,128)(2,1)S(1)}, bf16[2,2,16,1024]{3,2,1,0:T(8,128)(2,1)S(1)}, u32[]{:S(2)}, u32[]{:S(2)}) collective-permute-start(bf16[2,2,16,1024]{3,2,1,0:T(8,128)(2,1)S(1)} %add_convert_fusion.2), channel_id=1, source_target_pairs={{0,64},{16,80},{32,96},{48,112},{64,0},{80,16},{96,32},{112,48},{1... | collective-permute-start | bytes 393224 | tf_op jit(solution)/shard_map/ppermute | solution.py:167
  147.2 4.6 %copy-start.4 = (bf16[64,384,256]{2,1,0:T(8,128)(2,1)S(1)}, bf16[64,384,256]{2,1,0:T(8,128)(2,1)}, u32[]{:S(2)}) copy-start(bf16[64,384,256]{2,1,0:T(8,128)(2,1)} %reshape.47.basis_ref) | copy-start | bytes 37748740
  179.2 4.6 %copy-start.2 = (bf16[64,384,256]{2,1,0:T(8,128)(2,1)S(1)}, bf16[64,384,256]{2,1,0:T(8,128)(2,1)}, u32[]{:S(2)}) copy-start(bf16[64,384,256]{2,1,0:T(8,128)(2,1)} %reshape.43.basis_ref) | copy-start | bytes 37748740
  189.9 1.4 collective-permute-start.3
  191.4 5.6 %collective-permute-start.4 = (bf16[2,2,16,1024]{3,2,1,0:T(8,128)(2,1)S(1)}, bf16[2,2,16,1024]{3,2,1,0:T(8,128)(2,1)S(1)}, u32[]{:S(2)}, u32[]{:S(2)}) collective-permute-start(bf16[2,2,16,1024]{3,2,1,0:T(8,128)(2,1)S(1)} %add_convert_fusion.1), channel_id=1, source_target_pairs={{0,32},{16,48},{32,0},{48,16},{64,96},{80,112},{96,64},{112,80},{1... | collective-permute-start | bytes 393224 | tf_op jit(solution)/shard_map/ppermute | solution.py:167
  197.1 6.6 %collective-permute-start.5 = (bf16[2,2,16,1024]{3,2,1,0:T(8,128)(2,1)S(1)}, bf16[2,2,16,1024]{3,2,1,0:T(8,128)(2,1)S(1)}, u32[]{:S(2)}, u32[]{:S(2)}) collective-permute-start(bf16[2,2,16,1024]{3,2,1,0:T(8,128)(2,1)S(1)} %add_convert_fusion), channel_id=1, source_target_pairs={{0,64},{16,80},{32,96},{48,112},{64,0},{80,16},{96,32},{112,48},{1... | collective-permute-start | bytes 393224 | tf_op jit(solution)/shard_map/ppermute | solution.py:167
  203.7 34.4 %copy-start.7 = (f32[2,2,16,1024]{3,2,1,0:T(8,128)}, f32[2,2,16,1024]{3,2,1,0:T(8,128)S(1)}, u32[]{:S(2)}) copy-start(f32[2,2,16,1024]{3,2,1,0:T(8,128)S(1)} %multiply_subtract_fusion.model_ref) | copy-start | bytes 786436
  227.2 4.6 %copy-start.5 = (bf16[64,384,256]{2,1,0:T(8,128)(2,1)S(1)}, bf16[64,384,256]{2,1,0:T(8,128)(2,1)}, u32[]{:S(2)}) copy-start(bf16[64,384,256]{2,1,0:T(8,128)(2,1)} %reshape.47.basis_ref) | copy-start | bytes 37748740

commit v2 on v1

v2 whole, which is shorter than its diff:
```python
import math

import jax
import jax.numpy as jnp
from jax import lax
from jax.experimental import pallas as pl
from jax.experimental.pallas import tpu as pltpu
from jax.sharding import PartitionSpec as P

NV = 16
TILE = 256
RMAX = 96
F = 2
NT = 64
ITERS = 2
LANES = 128
HALVES = TILE // LANES
PAIRS = RMAX * 2
WIDE = F * PAIRS
ROWS = F * 2 * NV
GROUPS = 8
GROUP = 8

step_length = 0.8


def start_fetch(raw_ref, held_ref, sems):
    for group in range(GROUPS):
        for copy in fetches(raw_ref, held_ref, sems, group):
            copy.start()


def fetches(raw_ref, held_ref, sems, group):
    copies = []
    raw_ref = raw_ref.reshape(*raw_ref.shape[:-3], PAIRS, TILE)
    for half in range(HALVES):
        lanes = pl.ds(half * LANES, LANES)
        if len(raw_ref.shape) == 5:
            column, part = group // 2, group % 2
            source = raw_ref.at[pl.ds(part * GROUP, GROUP), column, :, :, lanes]
        else:
            source = raw_ref.at[pl.ds(group * GROUP, GROUP), :, :, lanes]
        copies.append(pltpu.make_async_copy(source, held_ref.at[half, group], sems.at[group, half]))
    return copies


def wait_fetch(raw_ref, held_ref, sems, group):
    for copy in fetches(raw_ref, held_ref, sems, group):
        copy.wait()


def lane_facts():
    lane = lax.broadcasted_iota(jnp.int32, (NV, WIDE), 1)
    first = lane < PAIRS
    rank = jnp.where(first, lane, lane - PAIRS) // 2
    return lane % 2 == 0, first, rank


def repeat_field(real, imag):
    return jnp.concatenate([real] * GROUP + [imag] * GROUP, axis=0).astype(jnp.bfloat16)


def project(wide_of, basis_ref, group):
    spot = lax.broadcasted_iota(jnp.int32, (PAIRS, LANES), 1) // NV
    even = lax.broadcasted_iota(jnp.int32, (PAIRS, LANES), 0) % 2 == 0
    blocks = []
    for f in range(F):
        rows = jnp.concatenate(
            [basis_ref[half, group, :, f].reshape(GROUP * PAIRS, LANES) for half in range(HALVES)], axis=1
        )
        z = lax.dot_general(rows, wide_of(f), (((1,), (1,)), ((), ())), preferred_element_type=jnp.float32)
        real, imag = z[0:PAIRS, :LANES], z[0:PAIRS, LANES:]
        for p in range(1, GROUP):
            here = spot == p
            real = jnp.where(here, z[p * PAIRS : (p + 1) * PAIRS, :LANES], real)
            imag = jnp.where(here, z[p * PAIRS : (p + 1) * PAIRS, LANES:], imag)
        ahead = pltpu.roll(imag, PAIRS - 1, 0)
        behind = pltpu.roll(imag, 1, 0)
        blocks.append(real + jnp.where(even, ahead, -behind))
    return jnp.concatenate(blocks, axis=0).T


def expand(packed, basis, even, first):
    wide = packed.astype(jnp.float32)
    ahead = pltpu.roll(wide, WIDE - 1, 1)
    behind = pltpu.roll(wide, 1, 1)
    swapped = jnp.where(even, -ahead, behind)
    zero = jnp.zeros_like(wide)
    left = jnp.concatenate(
        [
            jnp.where(first, wide, zero),
            jnp.where(first, swapped, zero),
            jnp.where(first, zero, wide),
            jnp.where(first, zero, swapped),
        ],
        axis=0,
    ).astype(jnp.bfloat16)
    return jnp.dot(left, basis, preferred_element_type=jnp.float32)


def tile_of(basis_ref, group, p):
    return jnp.concatenate([basis_ref[half, group, p].reshape(WIDE, LANES) for half in range(HALVES)], axis=1)


def rows_by_pair(held_ref):
    return held_ref


def forward_kernel(model_ref, raw_ref, ranks_ref, out_ref, held_ref, wide_ref, sems):
    start_fetch(raw_ref, held_ref, sems)
    basis_ref = rows_by_pair(held_ref)
    _, first, rank = lane_facts()
    for j in range(4):
        for f in range(F):
            real, imag = [model_ref[a, f, :, j * TILE : (j + 1) * TILE] for a in range(2)]
            wide_ref[j, f] = repeat_field(real, imag)

    def one(group, carry):
        wait_fetch(raw_ref, held_ref, sems, group)
        j = group // 2
        x = project(lambda f: wide_ref[j, f], basis_ref, group)
        for p in range(GROUP):
            tile = ((group % 2) * GROUP + p) * 4 + j
            limit = jnp.where(first, ranks_ref[tile, 0], ranks_ref[tile, 1])
            mine = jnp.where(rank < limit, x[p * NV : (p + 1) * NV], 0.0)
            out_ref[tile] = mine.astype(jnp.bfloat16)
        return carry

    lax.fori_loop(0, GROUPS, one, 0)


def gate(re0, im0, re1, im1, start, stop):
    outs = [jnp.zeros_like(re0) for _ in range(4)]
    for t in range(NT):
        rows = []
        for f in range(F):
            phase = 2.0 * math.pi * ((3 + 5 * f) * t % NT) / NT
            rows += [math.cos(phase), -math.sin(phase)]
        signal = re0 * rows[0] + im0 * rows[1] + re1 * rows[2] + im1 * rows[3]
        signal = jnp.where((start <= t) & (stop > t), signal, 0.0)
        outs = [o + signal * r for o, r in zip(outs, rows)]
    return [o * (2.0 / NT) for o in outs]


def residual_parts(got_ref, raw_ref, observed_ref, start_ref, stop_ref, held_ref, total_ref, sems):
    start_fetch(raw_ref, held_ref, sems)
    basis_ref = rows_by_pair(held_ref)
    even, first, _ = lane_facts()
    total_ref[...] = jnp.zeros_like(total_ref)

    def one(group, carry):
        wait_fetch(raw_ref, held_ref, sems, group)
        total = total_ref[...]
        for p in range(GROUP):
            total += expand(got_ref[group * GROUP + p], tile_of(basis_ref, group, p), even, first)
        total_ref[...] = total
        return carry

    lax.fori_loop(0, GROUPS, one, 0)
    parts = [
        total_ref[(2 * f + a) * NV : (2 * f + a + 1) * NV] - observed_ref[a, f] for f in range(F) for a in range(2)
    ]
    return gate(*parts, start_ref[...], stop_ref[...])


def middle_kernel(got_ref, raw_ref, observed_ref, start_ref, stop_ref, out_ref, held_ref, total_ref, wide_ref, sems):
    parts = residual_parts(got_ref, raw_ref, observed_ref, start_ref, stop_ref, held_ref, total_ref, sems)
    basis_ref = rows_by_pair(held_ref)
    for f in range(F):
        wide_ref[f] = repeat_field(parts[2 * f], parts[2 * f + 1])

    def one(group, carry):
        x = project(lambda f: wide_ref[f], basis_ref, group).astype(jnp.bfloat16)
        for p in range(GROUP):
            out_ref[group * GROUP + p] = x[p * NV : (p + 1) * NV]
        return carry

    lax.fori_loop(0, GROUPS, one, 0)


def last_kernel(got_ref, raw_ref, observed_ref, start_ref, stop_ref, out_ref, held_ref, total_ref, sems):
    parts = residual_parts(got_ref, raw_ref, observed_ref, start_ref, stop_ref, held_ref, total_ref, sems)
    for f in range(F):
        for a in range(2):
            out_ref[a, f] = parts[2 * f + a]


def gradient_kernel(got_ref, raw_ref, ranks_ref, out_ref, held_ref, sems):
    start_fetch(raw_ref, held_ref, sems)
    basis_ref = rows_by_pair(held_ref)
    even, first, rank = lane_facts()
    for j in range(4):

        def one(part, total):
            group = 2 * j + part
            wait_fetch(raw_ref, held_ref, sems, group)
            for p in range(GROUP):
                tile = (part * GROUP + p) * 4 + j
                limit = jnp.where(first, ranks_ref[tile, 0], ranks_ref[tile, 1])
                kept = jnp.where(rank < limit, got_ref[tile].astype(jnp.float32), 0.0)
                total += expand(kept, tile_of(basis_ref, group, p), even, first)
            return total

        total = lax.fori_loop(0, 2, one, jnp.zeros((ROWS, TILE), jnp.float32))
        for f in range(F):
            for a in range(2):
                row = (2 * f + a) * NV
                out_ref[a, f, :, j * TILE : (j + 1) * TILE] = total[row : row + NV]


VMEM = pl.BlockSpec(memory_space=pltpu.VMEM)
SMEM = pl.BlockSpec(memory_space=pltpu.SMEM)
HBM = pl.BlockSpec(memory_space=pltpu.HBM)
PACKED = jax.ShapeDtypeStruct((64, NV, WIDE), jnp.bfloat16)
HELD = pltpu.VMEM((HALVES, GROUPS, GROUP, F, PAIRS, LANES), jnp.bfloat16)
TOTAL = pltpu.VMEM((ROWS, TILE), jnp.float32)
SEMS = pltpu.SemaphoreType.DMA((GROUPS, HALVES))


def wide(*lead):
    return pltpu.VMEM((*lead, F, TILE, TILE), jnp.bfloat16)


def call(kernel, specs, out, scratch):
    return pl.pallas_call(
        kernel,
        out_shape=out,
        in_specs=specs,
        out_specs=VMEM,
        scratch_shapes=scratch,
        compiler_params=pltpu.CompilerParams(vmem_limit_bytes=40 * 1024 * 1024),
        name=kernel.__name__,
    )


def exchange(packed):
    parts = packed.reshape(16, 4, NV, WIDE)
    return lax.all_to_all(parts, "col", 0, 0, tiled=True).reshape(64, NV, WIDE)


def row_sum(local):
    low = local.astype(jnp.bfloat16).astype(jnp.float32)
    for step in (1, 2, 4):
        other = lax.ppermute(low.astype(jnp.bfloat16), "row", [(d, d ^ step) for d in range(8)])
        low = low.astype(jnp.bfloat16).astype(jnp.float32) + other.astype(jnp.float32)
    return low


def shards(model_init, observed, left_bases, right_bases, tile_ranks, gate_start, gate_stop):
    left = pltpu.with_memory_space_constraint(left_bases.reshape(left_bases.shape[1:]), pltpu.HBM)
    right = pltpu.with_memory_space_constraint(right_bases, pltpu.HBM)
    ranks = tile_ranks.reshape(64, F)
    forward = call(forward_kernel, [VMEM, HBM, SMEM], PACKED, [HELD, wide(4), SEMS])
    middle = call(middle_kernel, [VMEM, HBM] + [VMEM] * 3, PACKED, [HELD, TOTAL, wide(), SEMS])
    last = call(
        last_kernel,
        [VMEM, HBM] + [VMEM] * 3,
        jax.ShapeDtypeStruct((2, F, NV, TILE), jnp.float32),
        [HELD, TOTAL, SEMS],
    )
    gradient = call(
        gradient_kernel, [VMEM, HBM, SMEM], jax.ShapeDtypeStruct((2, F, NV, 1024), jnp.float32), [HELD, SEMS]
    )
    estimate = model_init
    for iteration in range(ITERS):
        got = exchange(forward(estimate, right, ranks))
        back = exchange(middle(got, left, observed, gate_start, gate_stop))
        estimate = estimate - step_length * row_sum(gradient(back, right, ranks))
    got = exchange(forward(estimate, right, ranks))
    return estimate, last(got, left, observed, gate_start, gate_stop)


def solution(mesh):
    placed = (
        P(None, None, None, "col"),
        P(None, None, None, ("row", "col")),
        P(("row", "col"), None, None, None, None, None),
        P("row", "col", None, None, None, None),
        P("row", "col", None),
        P(None, ("row", "col")),
        P(None, ("row", "col")),
    )
    return jax.shard_map(
        shards,
        mesh=mesh,
        in_specs=placed,
        out_specs=(P(None, None, None, "col"), P(None, None, None, ("row", "col"))),
        check_vma=False,
    )
```

time: 240 us -> 182 us (0.76)
  local copies, waits for them, and re-layouts: 66.4 us -> 1.77 us
  blocking collectives: 66.9 us -> 85.1 us
  starting transfers between devices: 17.7 us -> 9.52 us
    reshape x2 -> x0, local copies, waits for them, and re-layouts: 38.1 us -> none  [the longest x1 19.1 us: shards(): left = left_bases.reshape(64, WIDE, TILE)]
    unnamed x22 -> x12, local copies, waits for them, and re-layouts: 27.5 us -> 0.97 us
    all_to_all x4 -> x5, blocking collectives: 66.9 us -> 85.1 us  [exchange(): return lax.all_to_all(parts, 'col', 0, 0, tiled=True).reshape(64, NV, WIDE)]
    all_to_all x1 -> x0, starting transfers between devices: 8.16 us -> none  [exchange(): return lax.all_to_all(parts, 'col', 0, 0, tiled=True).reshape(64, NV, WIDE)]
  transfers between devices with their start and end apart: 7 -> 6, of which waited for: 6 -> 6; matrix products, arithmetic and copies ran while one was open for 8% -> 0% of each run, Pallas kernels for 0% -> 0%
where the time goes in v2:
time: 182 us
  blocking collectives  85.1 us (47%)
  Pallas kernels  67 us (37%)
  waiting for transfers between devices  17.7 us (10%)
  starting transfers between devices  9.52 us (5%)
    all_to_all x5, blocking collectives, exchange(): return lax.all_to_all(parts, 'col', 0, 0, tiled=True).reshape(64, NV, WIDE)  85.1 us
    pallas_call x3, Pallas kernels, shards(): got = exchange(forward(estimate, right, ranks))  25 us
    pallas_call x2, Pallas kernels, shards(): back = exchange(middle(got, left, observed, gate_start, gate_stop))  23 us
    ppermute x6, waiting for transfers between devices, row_sum(): lax.ppermute(low.astype(jnp.bfloat16), 'row', [(d, d ^ step) for d in ran...  17.7 us
    pallas_call x2, Pallas kernels, shards(): estimate = estimate - step_length * row_sum(gradient(back, right, ranks))  12.5 us
    ppermute x6, starting transfers between devices, row_sum(): lax.ppermute(low.astype(jnp.bfloat16), 'row', [(d, d ^ step) for d in ran...  9.52 us
    pallas_call x1, Pallas kernels, shards(): return (estimate, last(got, left, observed, gate_start, gate_stop))  6.39 us
  transfers between devices with their start and end apart: 6, of which 6 were waited for; matrix products, arithmetic and copies ran while one was open for 0% of the time, Pallas kernels for 0%

profile of v2, /device:TPU:0, one launch (start us, length us, event | category | flops | bytes accessed | tf_op | source)
XLA Modules:
  0.0 182.1 jit_solution(7480733041114172681)
XLA Ops:
  0.6 0.0 copy-start.5
  0.6 0.0 copy-start.4
  0.7 0.8 copy.21
  1.4 0.0 copy-start
  1.5 0.9 copy-done
  2.4 0.0 copy-start.3
  2.4 8.3 %forward_kernel.3 = bf16[64,16,384]{2,1,0:T(8,128)(2,1)S(1)} custom-call(f32[2,2,16,1024]{3,2,1,0:T(8,128)S(1)} %copy-done, bf16[16,4,2,96,2,256]{5,4,3,2,1,0:T(2,128)(2,1)} %raw_ref.9, s32[64,2]{1,0:T(8,128)S(1)} %bitcast.22), custom_call_target="tpu_custom_call" | custom-call | tf_op jit(solution)/shard_map/forward_kernel/pallas_call | solution.py:266
  10.8 22.3 %all_to_all.25 = bf16[16,4,16,384]{3,2,1,0:T(8,128)(2,1)S(1)} all-to-all(bf16[16,4,16,384]{3,2,1,0:T(8,128)(2,1)S(1)} %bitcast.20), channel_id=1, replica_groups=mesh['row'=8,'col'=16] {'col'}, dimensions={0} | all-to-all | bytes 1572864 | tf_op jit(solution)/shard_map/all_to_all | solution.py:238
  33.1 0.0 copy-done.5
  33.1 0.0 copy-done.4
  33.1 0.0 copy-done.3
  33.1 0.0 copy-start.1
  33.1 11.5 %middle_kernel.2 = bf16[64,16,384]{2,1,0:T(8,128)(2,1)S(1)} custom-call(bf16[64,16,384]{2,1,0:T(8,128)(2,1)S(1)} %bitcast.12, bf16[64,2,96,2,256]{4,3,2,1,0:T(2,128)(2,1)} %bitcast.27, f32[2,2,16,256]{3,2,1,0:T(8,128)S(1)} %copy-done.3, s32[16,256]{1,0:T(8,128)S(1)} %copy-done.4, s32[16,256]{1,0:T(8,128)S(1)} %copy-done.5), custom_call_target="tpu_custom_call" | custom-call | tf_op jit(solution)/shard_map/middle_kernel/pallas_call | solution.py:267
  44.6 16.7 %all_to_all.26 = bf16[16,4,16,384]{3,2,1,0:T(8,128)(2,1)S(1)} all-to-all(bf16[16,4,16,384]{3,2,1,0:T(8,128)(2,1)S(1)} %bitcast.13), channel_id=1, replica_groups=mesh['row'=8,'col'=16] {'col'}, dimensions={0} | all-to-all | bytes 1572864 | tf_op jit(solution)/shard_map/all_to_all | solution.py:238
  61.3 6.3 %gradient_kernel.2 = f32[2,2,16,1024]{3,2,1,0:T(8,128)S(1)} custom-call(bf16[64,16,384]{2,1,0:T(8,128)(2,1)S(1)} %bitcast.17, bf16[16,4,2,96,2,256]{5,4,3,2,1,0:T(2,128)(2,1)} %raw_ref.9, s32[64,2]{1,0:T(8,128)S(1)} %bitcast.23), custom_call_target="tpu_custom_call" | custom-call | tf_op jit(solution)/shard_map/gradient_kernel/pallas_call | solution.py:268
  67.6 0.1 collective-permute-start
  67.7 1.3 collective-permute-done
  69.0 1.6 collective-permute-start.1
  70.6 4.1 %collective-permute-done.1 = bf16[2,2,16,1024]{3,2,1,0:T(8,128)(2,1)S(1)} collective-permute-done((bf16[2,2,16,1024]{3,2,1,0:T(8,128)(2,1)S(1)}, bf16[2,2,16,1024]{3,2,1,0:T(8,128)(2,1)S(1)}, u32[]{:S(2)}, u32[]{:S(2)}) %collective-permute-start.1) | collective-permute-done | bytes 131104 | tf_op jit(solution)/shard_map/ppermute | solution.py:244
  74.7 3.1 %collective-permute-start.2 = (bf16[2,2,16,1024]{3,2,1,0:T(8,128)(2,1)S(1)}, bf16[2,2,16,1024]{3,2,1,0:T(8,128)(2,1)S(1)}, u32[]{:S(2)}, u32[]{:S(2)}) collective-permute-start(bf16[2,2,16,1024]{3,2,1,0:T(8,128)(2,1)S(1)} %add_convert_fusion.2), channel_id=1, source_target_pairs={{0,64},{16,80},{32,96},{48,112},{64,0},{80,16},{96,32},{112,48},{1... | collective-permute-start | bytes 393224 | tf_op jit(solution)/shard_map/ppermute | solution.py:244
  77.8 3.5 %collective-permute-done.2 = bf16[2,2,16,1024]{3,2,1,0:T(8,128)(2,1)S(1)} collective-permute-done((bf16[2,2,16,1024]{3,2,1,0:T(8,128)(2,1)S(1)}, bf16[2,2,16,1024]{3,2,1,0:T(8,128)(2,1)S(1)}, u32[]{:S(2)}, u32[]{:S(2)}) %collective-permute-start.2) | collective-permute-done | bytes 131104 | tf_op jit(solution)/shard_map/ppermute | solution.py:244
  81.3 0.0 copy-done.1
  81.3 8.3 %forward_kernel.4 = bf16[64,16,384]{2,1,0:T(8,128)(2,1)S(1)} custom-call(f32[2,2,16,1024]{3,2,1,0:T(8,128)S(1)} %multiply_subtract_fusion.1.model_ref, bf16[16,4,2,96,2,256]{5,4,3,2,1,0:T(2,128)(2,1)} %raw_ref.9, s32[64,2]{1,0:T(8,128)S(1)} %bitcast.24), custom_call_target="tpu_custom_call" | custom-call | tf_op jit(solution)/shard_map/forward_kernel/pallas_call | solution.py:266
  89.7 15.6 %all_to_all.27 = bf16[16,4,16,384]{3,2,1,0:T(8,128)(2,1)S(1)} all-to-all(bf16[16,4,16,384]{3,2,1,0:T(8,128)(2,1)S(1)} %bitcast.21), channel_id=1, replica_groups=mesh['row'=8,'col'=16] {'col'}, dimensions={0} | all-to-all | bytes 1572864 | tf_op jit(solution)/shard_map/all_to_all | solution.py:238
  105.3 11.5 %middle_kernel.3 = bf16[64,16,384]{2,1,0:T(8,128)(2,1)S(1)} custom-call(bf16[64,16,384]{2,1,0:T(8,128)(2,1)S(1)} %bitcast.14, bf16[64,2,96,2,256]{4,3,2,1,0:T(2,128)(2,1)} %bitcast.28, f32[2,2,16,256]{3,2,1,0:T(8,128)S(1)} %copy-done.3, s32[16,256]{1,0:T(8,128)S(1)} %copy-done.4, s32[16,256]{1,0:T(8,128)S(1)} %copy-done.5), custom_call_target="tpu_custom_call" | custom-call | tf_op jit(solution)/shard_map/middle_kernel/pallas_call | solution.py:267
  116.8 14.9 %all_to_all.28 = bf16[16,4,16,384]{3,2,1,0:T(8,128)(2,1)S(1)} all-to-all(bf16[16,4,16,384]{3,2,1,0:T(8,128)(2,1)S(1)} %bitcast.15), channel_id=1, replica_groups=mesh['row'=8,'col'=16] {'col'}, dimensions={0} | all-to-all | bytes 1572864 | tf_op jit(solution)/shard_map/all_to_all | solution.py:238
  131.7 6.3 %gradient_kernel.3 = f32[2,2,16,1024]{3,2,1,0:T(8,128)S(1)} custom-call(bf16[64,16,384]{2,1,0:T(8,128)(2,1)S(1)} %bitcast.18, bf16[16,4,2,96,2,256]{5,4,3,2,1,0:T(2,128)(2,1)} %raw_ref.9, s32[64,2]{1,0:T(8,128)S(1)} %bitcast.25), custom_call_target="tpu_custom_call" | custom-call | tf_op jit(solution)/shard_map/gradient_kernel/pallas_call | solution.py:268
  138.0 0.1 collective-permute-start.3
  138.1 1.3 collective-permute-done.3
  139.5 1.6 collective-permute-start.4
  141.1 4.1 %collective-permute-done.4 = bf16[2,2,16,1024]{3,2,1,0:T(8,128)(2,1)S(1)} collective-permute-done((bf16[2,2,16,1024]{3,2,1,0:T(8,128)(2,1)S(1)}, bf16[2,2,16,1024]{3,2,1,0:T(8,128)(2,1)S(1)}, u32[]{:S(2)}, u32[]{:S(2)}) %collective-permute-start.4) | collective-permute-done | bytes 131104 | tf_op jit(solution)/shard_map/ppermute | solution.py:244
  145.2 3.1 %collective-permute-start.5 = (bf16[2,2,16,1024]{3,2,1,0:T(8,128)(2,1)S(1)}, bf16[2,2,16,1024]{3,2,1,0:T(8,128)(2,1)S(1)}, u32[]{:S(2)}, u32[]{:S(2)}) collective-permute-start(bf16[2,2,16,1024]{3,2,1,0:T(8,128)(2,1)S(1)} %add_convert_fusion), channel_id=1, source_target_pairs={{0,64},{16,80},{32,96},{48,112},{64,0},{80,16},{96,32},{112,48},{1... | collective-permute-start | bytes 393224 | tf_op jit(solution)/shard_map/ppermute | solution.py:244
  148.3 3.5 %collective-permute-done.5 = bf16[2,2,16,1024]{3,2,1,0:T(8,128)(2,1)S(1)} collective-permute-done((bf16[2,2,16,1024]{3,2,1,0:T(8,128)(2,1)S(1)}, bf16[2,2,16,1024]{3,2,1,0:T(8,128)(2,1)S(1)}, u32[]{:S(2)}, u32[]{:S(2)}) %collective-permute-start.5) | collective-permute-done | bytes 131104 | tf_op jit(solution)/shard_map/ppermute | solution.py:244
  151.8 0.0 copy-start.2
  151.8 8.3 %forward_kernel.5 = bf16[64,16,384]{2,1,0:T(8,128)(2,1)S(1)} custom-call(f32[2,2,16,1024]{3,2,1,0:T(8,128)S(1)} %multiply_subtract_fusion.model_ref, bf16[16,4,2,96,2,256]{5,4,3,2,1,0:T(2,128)(2,1)} %raw_ref.9, s32[64,2]{1,0:T(8,128)S(1)} %bitcast.26), custom_call_target="tpu_custom_call" | custom-call | tf_op jit(solution)/shard_map/forward_kernel/pallas_call | solution.py:269
  160.1 15.6 %all_to_all.29 = bf16[16,4,16,384]{3,2,1,0:T(8,128)(2,1)S(1)} all-to-all(bf16[16,4,16,384]{3,2,1,0:T(8,128)(2,1)S(1)} %bitcast.19), channel_id=1, replica_groups=mesh['row'=8,'col'=16] {'col'}, dimensions={0} | all-to-all | bytes 1572864 | tf_op jit(solution)/shard_map/all_to_all | solution.py:238
  175.7 6.4 %last_kernel.1 = f32[2,2,16,256]{3,2,1,0:T(8,128)} custom-call(bf16[64,16,384]{2,1,0:T(8,128)(2,1)S(1)} %bitcast.16, bf16[64,2,96,2,256]{4,3,2,1,0:T(2,128)(2,1)} %bitcast.29, f32[2,2,16,256]{3,2,1,0:T(8,128)S(1)} %copy-done.3, s32[16,256]{1,0:T(8,128)S(1)} %copy-done.4, s32[16,256]{1,0:T(8,128)S(1)} %copy-done.5), custom_call_target="tpu_custom_call" | custom-call | tf_op jit(solution)/shard_map/last_kernel/pallas_call | solution.py:270
  182.1 0.0 copy-done.2
  (8 shorter events, 0.2 us)
Async XLA Ops:
  0.6 32.4 %copy-start.5 = (s32[16,256]{1,0:T(8,128)S(1)}, s32[16,256]{1,0:T(8,128)}, u32[]{:S(2)}) copy-start(s32[16,256]{1,0:T(8,128)} %stop_ref.5) | copy-start | bytes 49156
  0.6 32.4 %copy-start.4 = (s32[16,256]{1,0:T(8,128)S(1)}, s32[16,256]{1,0:T(8,128)}, u32[]{:S(2)}) copy-start(s32[16,256]{1,0:T(8,128)} %start_ref.5) | copy-start | bytes 49156
  1.4 0.9 copy-start
  2.4 30.7 %copy-start.3 = (f32[2,2,16,256]{3,2,1,0:T(8,128)S(1)}, f32[2,2,16,256]{3,2,1,0:T(8,128)}, u32[]{:S(2)}) copy-start(f32[2,2,16,256]{3,2,1,0:T(8,128)} %observed_ref.5) | copy-start | bytes 196612
  33.1 48.2 %copy-start.1 = (f32[2,2,16,1024]{3,2,1,0:T(8,128)S(1)}, f32[2,2,16,1024]{3,2,1,0:T(8,128)}, u32[]{:S(2)}) copy-start(f32[2,2,16,1024]{3,2,1,0:T(8,128)} %model_ref.1) | copy-start | bytes 786436
  67.6 1.4 collective-permute-start
  69.0 5.6 %collective-permute-start.1 = (bf16[2,2,16,1024]{3,2,1,0:T(8,128)(2,1)S(1)}, bf16[2,2,16,1024]{3,2,1,0:T(8,128)(2,1)S(1)}, u32[]{:S(2)}, u32[]{:S(2)}) collective-permute-start(bf16[2,2,16,1024]{3,2,1,0:T(8,128)(2,1)S(1)} %add_convert_fusion.3), channel_id=1, source_target_pairs={{0,32},{16,48},{32,0},{48,16},{64,96},{80,112},{96,64},{112,80},{1... | collective-permute-start | bytes 393224 | tf_op jit(solution)/shard_map/ppermute | solution.py:244
  74.7 6.6 %collective-permute-start.2 = (bf16[2,2,16,1024]{3,2,1,0:T(8,128)(2,1)S(1)}, bf16[2,2,16,1024]{3,2,1,0:T(8,128)(2,1)S(1)}, u32[]{:S(2)}, u32[]{:S(2)}) collective-permute-start(bf16[2,2,16,1024]{3,2,1,0:T(8,128)(2,1)S(1)} %add_convert_fusion.2), channel_id=1, source_target_pairs={{0,64},{16,80},{32,96},{48,112},{64,0},{80,16},{96,32},{112,48},{1... | collective-permute-start | bytes 393224 | tf_op jit(solution)/shard_map/ppermute | solution.py:244
  138.0 1.4 collective-permute-start.3
  139.5 5.6 %collective-permute-start.4 = (bf16[2,2,16,1024]{3,2,1,0:T(8,128)(2,1)S(1)}, bf16[2,2,16,1024]{3,2,1,0:T(8,128)(2,1)S(1)}, u32[]{:S(2)}, u32[]{:S(2)}) collective-permute-start(bf16[2,2,16,1024]{3,2,1,0:T(8,128)(2,1)S(1)} %add_convert_fusion.1), channel_id=1, source_target_pairs={{0,32},{16,48},{32,0},{48,16},{64,96},{80,112},{96,64},{112,80},{1... | collective-permute-start | bytes 393224 | tf_op jit(solution)/shard_map/ppermute | solution.py:244
  145.2 6.6 %collective-permute-start.5 = (bf16[2,2,16,1024]{3,2,1,0:T(8,128)(2,1)S(1)}, bf16[2,2,16,1024]{3,2,1,0:T(8,128)(2,1)S(1)}, u32[]{:S(2)}, u32[]{:S(2)}) collective-permute-start(bf16[2,2,16,1024]{3,2,1,0:T(8,128)(2,1)S(1)} %add_convert_fusion), channel_id=1, source_target_pairs={{0,64},{16,80},{32,96},{48,112},{64,0},{80,16},{96,32},{112,48},{1... | collective-permute-start | bytes 393224 | tf_op jit(solution)/shard_map/ppermute | solution.py:244
  151.8 30.4 %copy-start.2 = (f32[2,2,16,1024]{3,2,1,0:T(8,128)}, f32[2,2,16,1024]{3,2,1,0:T(8,128)S(1)}, u32[]{:S(2)}) copy-start(f32[2,2,16,1024]{3,2,1,0:T(8,128)S(1)} %multiply_subtract_fusion.model_ref) | copy-start | bytes 786436

commit v3 on v2

--- a/solution.py
+++ b/solution.py
@@ -57,7 +57,7 @@
 
 
 def repeat_field(real, imag):
-    return jnp.concatenate([real] * GROUP + [imag] * GROUP, axis=0).astype(jnp.bfloat16)
+    return jnp.concatenate([real] * GROUP + [imag] * GROUP, axis=0).T.astype(jnp.bfloat16)
 
 
 def project(wide_of, basis_ref, group):
@@ -68,7 +68,7 @@
         rows = jnp.concatenate(
             [basis_ref[half, group, :, f].reshape(GROUP * PAIRS, LANES) for half in range(HALVES)], axis=1
         )
-        z = lax.dot_general(rows, wide_of(f), (((1,), (1,)), ((), ())), preferred_element_type=jnp.float32)
+        z = jnp.dot(rows, wide_of(f), preferred_element_type=jnp.float32)
         real, imag = z[0:PAIRS, :LANES], z[0:PAIRS, LANES:]
         for p in range(1, GROUP):
             here = spot == p
@@ -126,7 +126,7 @@
             out_ref[tile] = mine.astype(jnp.bfloat16)
         return carry
 
-    lax.fori_loop(0, GROUPS, one, 0)
+    lax.fori_loop(0, GROUPS, one, 0, unroll=2)
 
 
 def gate(re0, im0, re1, im1, start, stop):
@@ -175,7 +175,7 @@
             out_ref[group * GROUP + p] = x[p * NV : (p + 1) * NV]
         return carry
 
-    lax.fori_loop(0, GROUPS, one, 0)
+    lax.fori_loop(0, GROUPS, one, 0, unroll=2)
 
 
 def last_kernel(got_ref, raw_ref, observed_ref, start_ref, stop_ref, out_ref, held_ref, total_ref, sems):
@@ -240,7 +240,7 @@
 
 def row_sum(local):
     low = local.astype(jnp.bfloat16).astype(jnp.float32)
-    for step in (1, 2, 4):
+    for step in (1, 2, 6):
         other = lax.ppermute(low.astype(jnp.bfloat16), "row", [(d, d ^ step) for d in range(8)])
         low = low.astype(jnp.bfloat16).astype(jnp.float32) + other.astype(jnp.float32)
     return low

time: 182 us -> 179 us (0.984)
  Pallas kernels: 67 us -> 63.8 us
    pallas_call x2, Pallas kernels: 23 us -> 20.7 us  [shards(): back = exchange(middle(got, left, observed, gate_start, gate_stop))]
where the time goes in v3:
time: 179 us
  blocking collectives  85.1 us (48%)
  Pallas kernels  63.8 us (36%)
  waiting for transfers between devices  18.8 us (11%)
  starting transfers between devices  7.77 us (4%)
    all_to_all x5, blocking collectives, exchange(): return lax.all_to_all(parts, 'col', 0, 0, tiled=True).reshape(64, NV, WIDE)  85.1 us
    pallas_call x3, Pallas kernels, shards(): got = exchange(forward(estimate, right, ranks))  24.2 us
    pallas_call x2, Pallas kernels, shards(): back = exchange(middle(got, left, observed, gate_start, gate_stop))  20.7 us
    ppermute x6, waiting for transfers between devices, row_sum(): lax.ppermute(low.astype(jnp.bfloat16), 'row', [(d, d ^ step) for d in ran...  18.8 us
    pallas_call x2, Pallas kernels, shards(): estimate = estimate - step_length * row_sum(gradient(back, right, ranks))  12.5 us
    ppermute x6, starting transfers between devices, row_sum(): lax.ppermute(low.astype(jnp.bfloat16), 'row', [(d, d ^ step) for d in ran...  7.77 us
    pallas_call x1, Pallas kernels, shards(): return (estimate, last(got, left, observed, gate_start, gate_stop))  6.39 us
  transfers between devices with their start and end apart: 6, of which 6 were waited for; matrix products, arithmetic and copies ran while one was open for 0% of the time, Pallas kernels for 0%

profile of v3, /device:TPU:0, one launch (start us, length us, event | category | flops | bytes accessed | tf_op | source)
XLA Modules:
  0.0 178.5 jit_solution(16497826264076067544)
XLA Ops:
  0.6 0.0 copy-start.5
  0.6 0.0 copy-start.4
  0.7 0.8 copy.21
  1.4 0.0 copy-start
  1.5 0.9 copy-done
  2.4 0.0 copy-start.3
  2.4 8.1 %forward_kernel.3 = bf16[64,16,384]{2,1,0:T(8,128)(2,1)S(1)} custom-call(f32[2,2,16,1024]{3,2,1,0:T(8,128)S(1)} %copy-done, bf16[16,4,2,96,2,256]{5,4,3,2,1,0:T(2,128)(2,1)} %raw_ref.9, s32[64,2]{1,0:T(8,128)S(1)} %bitcast.22), custom_call_target="tpu_custom_call" | custom-call | tf_op jit(solution)/shard_map/forward_kernel/pallas_call | solution.py:266
  10.5 22.3 %all_to_all.25 = bf16[16,4,16,384]{3,2,1,0:T(8,128)(2,1)S(1)} all-to-all(bf16[16,4,16,384]{3,2,1,0:T(8,128)(2,1)S(1)} %bitcast.20), channel_id=1, replica_groups=mesh['row'=8,'col'=16] {'col'}, dimensions={0} | all-to-all | bytes 1572864 | tf_op jit(solution)/shard_map/all_to_all | solution.py:238
  32.8 0.0 copy-done.5
  32.8 0.0 copy-done.4
  32.8 0.0 copy-done.3
  32.8 0.0 copy-start.1
  32.8 10.4 %middle_kernel.2 = bf16[64,16,384]{2,1,0:T(8,128)(2,1)S(1)} custom-call(bf16[64,16,384]{2,1,0:T(8,128)(2,1)S(1)} %bitcast.12, bf16[64,2,96,2,256]{4,3,2,1,0:T(2,128)(2,1)} %bitcast.27, f32[2,2,16,256]{3,2,1,0:T(8,128)S(1)} %copy-done.3, s32[16,256]{1,0:T(8,128)S(1)} %copy-done.4, s32[16,256]{1,0:T(8,128)S(1)} %copy-done.5), custom_call_target="tpu_custom_call" | custom-call | tf_op jit(solution)/shard_map/middle_kernel/pallas_call | solution.py:267
  43.2 16.7 %all_to_all.26 = bf16[16,4,16,384]{3,2,1,0:T(8,128)(2,1)S(1)} all-to-all(bf16[16,4,16,384]{3,2,1,0:T(8,128)(2,1)S(1)} %bitcast.13), channel_id=1, replica_groups=mesh['row'=8,'col'=16] {'col'}, dimensions={0} | all-to-all | bytes 1572864 | tf_op jit(solution)/shard_map/all_to_all | solution.py:238
  59.9 6.3 %gradient_kernel.2 = f32[2,2,16,1024]{3,2,1,0:T(8,128)S(1)} custom-call(bf16[64,16,384]{2,1,0:T(8,128)(2,1)S(1)} %bitcast.17, bf16[16,4,2,96,2,256]{5,4,3,2,1,0:T(2,128)(2,1)} %raw_ref.9, s32[64,2]{1,0:T(8,128)S(1)} %bitcast.23), custom_call_target="tpu_custom_call" | custom-call | tf_op jit(solution)/shard_map/gradient_kernel/pallas_call | solution.py:268
  66.1 0.1 collective-permute-start
  66.2 1.3 collective-permute-done
  67.6 1.6 collective-permute-start.1
  69.2 4.1 %collective-permute-done.1 = bf16[2,2,16,1024]{3,2,1,0:T(8,128)(2,1)S(1)} collective-permute-done((bf16[2,2,16,1024]{3,2,1,0:T(8,128)(2,1)S(1)}, bf16[2,2,16,1024]{3,2,1,0:T(8,128)(2,1)S(1)}, u32[]{:S(2)}, u32[]{:S(2)}) %collective-permute-start.1) | collective-permute-done | bytes 131104 | tf_op jit(solution)/shard_map/ppermute | solution.py:244
  73.3 2.8 %collective-permute-start.2 = (bf16[2,2,16,1024]{3,2,1,0:T(8,128)(2,1)S(1)}, bf16[2,2,16,1024]{3,2,1,0:T(8,128)(2,1)S(1)}, u32[]{:S(2)}, u32[]{:S(2)}) collective-permute-start(bf16[2,2,16,1024]{3,2,1,0:T(8,128)(2,1)S(1)} %add_convert_fusion.2), channel_id=1, source_target_pairs={{0,96},{16,112},{32,64},{48,80},{64,32},{80,48},{96,0},{112,16},{1... | collective-permute-start | bytes 393224 | tf_op jit(solution)/shard_map/ppermute | solution.py:244
  76.1 3.4 %collective-permute-done.2 = bf16[2,2,16,1024]{3,2,1,0:T(8,128)(2,1)S(1)} collective-permute-done((bf16[2,2,16,1024]{3,2,1,0:T(8,128)(2,1)S(1)}, bf16[2,2,16,1024]{3,2,1,0:T(8,128)(2,1)S(1)}, u32[]{:S(2)}, u32[]{:S(2)}) %collective-permute-start.2) | collective-permute-done | bytes 131104 | tf_op jit(solution)/shard_map/ppermute | solution.py:244
  79.5 0.0 copy-done.1
  79.6 8.1 %forward_kernel.4 = bf16[64,16,384]{2,1,0:T(8,128)(2,1)S(1)} custom-call(f32[2,2,16,1024]{3,2,1,0:T(8,128)S(1)} %multiply_subtract_fusion.1.model_ref, bf16[16,4,2,96,2,256]{5,4,3,2,1,0:T(2,128)(2,1)} %raw_ref.9, s32[64,2]{1,0:T(8,128)S(1)} %bitcast.24), custom_call_target="tpu_custom_call" | custom-call | tf_op jit(solution)/shard_map/forward_kernel/pallas_call | solution.py:266
  87.7 15.6 %all_to_all.27 = bf16[16,4,16,384]{3,2,1,0:T(8,128)(2,1)S(1)} all-to-all(bf16[16,4,16,384]{3,2,1,0:T(8,128)(2,1)S(1)} %bitcast.21), channel_id=1, replica_groups=mesh['row'=8,'col'=16] {'col'}, dimensions={0} | all-to-all | bytes 1572864 | tf_op jit(solution)/shard_map/all_to_all | solution.py:238
  103.3 10.3 %middle_kernel.3 = bf16[64,16,384]{2,1,0:T(8,128)(2,1)S(1)} custom-call(bf16[64,16,384]{2,1,0:T(8,128)(2,1)S(1)} %bitcast.14, bf16[64,2,96,2,256]{4,3,2,1,0:T(2,128)(2,1)} %bitcast.28, f32[2,2,16,256]{3,2,1,0:T(8,128)S(1)} %copy-done.3, s32[16,256]{1,0:T(8,128)S(1)} %copy-done.4, s32[16,256]{1,0:T(8,128)S(1)} %copy-done.5), custom_call_target="tpu_custom_call" | custom-call | tf_op jit(solution)/shard_map/middle_kernel/pallas_call | solution.py:267
  113.6 14.9 %all_to_all.28 = bf16[16,4,16,384]{3,2,1,0:T(8,128)(2,1)S(1)} all-to-all(bf16[16,4,16,384]{3,2,1,0:T(8,128)(2,1)S(1)} %bitcast.15), channel_id=1, replica_groups=mesh['row'=8,'col'=16] {'col'}, dimensions={0} | all-to-all | bytes 1572864 | tf_op jit(solution)/shard_map/all_to_all | solution.py:238
  128.6 6.3 %gradient_kernel.3 = f32[2,2,16,1024]{3,2,1,0:T(8,128)S(1)} custom-call(bf16[64,16,384]{2,1,0:T(8,128)(2,1)S(1)} %bitcast.18, bf16[16,4,2,96,2,256]{5,4,3,2,1,0:T(2,128)(2,1)} %raw_ref.9, s32[64,2]{1,0:T(8,128)S(1)} %bitcast.25), custom_call_target="tpu_custom_call" | custom-call | tf_op jit(solution)/shard_map/gradient_kernel/pallas_call | solution.py:268
  134.8 0.1 collective-permute-start.3
  134.9 1.3 collective-permute-done.3
  136.3 0.4 collective-permute-start.4
  136.7 5.3 %collective-permute-done.4 = bf16[2,2,16,1024]{3,2,1,0:T(8,128)(2,1)S(1)} collective-permute-done((bf16[2,2,16,1024]{3,2,1,0:T(8,128)(2,1)S(1)}, bf16[2,2,16,1024]{3,2,1,0:T(8,128)(2,1)S(1)}, u32[]{:S(2)}, u32[]{:S(2)}) %collective-permute-start.4) | collective-permute-done | bytes 131104 | tf_op jit(solution)/shard_map/ppermute | solution.py:244
  142.0 2.8 %collective-permute-start.5 = (bf16[2,2,16,1024]{3,2,1,0:T(8,128)(2,1)S(1)}, bf16[2,2,16,1024]{3,2,1,0:T(8,128)(2,1)S(1)}, u32[]{:S(2)}, u32[]{:S(2)}) collective-permute-start(bf16[2,2,16,1024]{3,2,1,0:T(8,128)(2,1)S(1)} %add_convert_fusion), channel_id=1, source_target_pairs={{0,96},{16,112},{32,64},{48,80},{64,32},{80,48},{96,0},{112,16},{1... | collective-permute-start | bytes 393224 | tf_op jit(solution)/shard_map/ppermute | solution.py:244
  144.8 3.4 %collective-permute-done.5 = bf16[2,2,16,1024]{3,2,1,0:T(8,128)(2,1)S(1)} collective-permute-done((bf16[2,2,16,1024]{3,2,1,0:T(8,128)(2,1)S(1)}, bf16[2,2,16,1024]{3,2,1,0:T(8,128)(2,1)S(1)}, u32[]{:S(2)}, u32[]{:S(2)}) %collective-permute-start.5) | collective-permute-done | bytes 131104 | tf_op jit(solution)/shard_map/ppermute | solution.py:244
  148.3 0.0 copy-start.2
  148.3 8.1 %forward_kernel.5 = bf16[64,16,384]{2,1,0:T(8,128)(2,1)S(1)} custom-call(f32[2,2,16,1024]{3,2,1,0:T(8,128)S(1)} %multiply_subtract_fusion.model_ref, bf16[16,4,2,96,2,256]{5,4,3,2,1,0:T(2,128)(2,1)} %raw_ref.9, s32[64,2]{1,0:T(8,128)S(1)} %bitcast.26), custom_call_target="tpu_custom_call" | custom-call | tf_op jit(solution)/shard_map/forward_kernel/pallas_call | solution.py:269
  156.4 15.6 %all_to_all.29 = bf16[16,4,16,384]{3,2,1,0:T(8,128)(2,1)S(1)} all-to-all(bf16[16,4,16,384]{3,2,1,0:T(8,128)(2,1)S(1)} %bitcast.19), channel_id=1, replica_groups=mesh['row'=8,'col'=16] {'col'}, dimensions={0} | all-to-all | bytes 1572864 | tf_op jit(solution)/shard_map/all_to_all | solution.py:238
  172.0 6.4 %last_kernel.1 = f32[2,2,16,256]{3,2,1,0:T(8,128)} custom-call(bf16[64,16,384]{2,1,0:T(8,128)(2,1)S(1)} %bitcast.16, bf16[64,2,96,2,256]{4,3,2,1,0:T(2,128)(2,1)} %bitcast.29, f32[2,2,16,256]{3,2,1,0:T(8,128)S(1)} %copy-done.3, s32[16,256]{1,0:T(8,128)S(1)} %copy-done.4, s32[16,256]{1,0:T(8,128)S(1)} %copy-done.5), custom_call_target="tpu_custom_call" | custom-call | tf_op jit(solution)/shard_map/last_kernel/pallas_call | solution.py:270
  178.4 0.0 copy-done.2
  (8 shorter events, 0.2 us)
Async XLA Ops:
  0.6 32.1 %copy-start.5 = (s32[16,256]{1,0:T(8,128)S(1)}, s32[16,256]{1,0:T(8,128)}, u32[]{:S(2)}) copy-start(s32[16,256]{1,0:T(8,128)} %stop_ref.5) | copy-start | bytes 49156
  0.6 32.1 %copy-start.4 = (s32[16,256]{1,0:T(8,128)S(1)}, s32[16,256]{1,0:T(8,128)}, u32[]{:S(2)}) copy-start(s32[16,256]{1,0:T(8,128)} %start_ref.5) | copy-start | bytes 49156
  1.4 0.9 copy-start
  2.4 30.4 %copy-start.3 = (f32[2,2,16,256]{3,2,1,0:T(8,128)S(1)}, f32[2,2,16,256]{3,2,1,0:T(8,128)}, u32[]{:S(2)}) copy-start(f32[2,2,16,256]{3,2,1,0:T(8,128)} %observed_ref.5) | copy-start | bytes 196612
  32.8 46.7 %copy-start.1 = (f32[2,2,16,1024]{3,2,1,0:T(8,128)S(1)}, f32[2,2,16,1024]{3,2,1,0:T(8,128)}, u32[]{:S(2)}) copy-start(f32[2,2,16,1024]{3,2,1,0:T(8,128)} %model_ref.1) | copy-start | bytes 786436
  66.1 1.4 collective-permute-start
  67.6 5.6 %collective-permute-start.1 = (bf16[2,2,16,1024]{3,2,1,0:T(8,128)(2,1)S(1)}, bf16[2,2,16,1024]{3,2,1,0:T(8,128)(2,1)S(1)}, u32[]{:S(2)}, u32[]{:S(2)}) collective-permute-start(bf16[2,2,16,1024]{3,2,1,0:T(8,128)(2,1)S(1)} %add_convert_fusion.3), channel_id=1, source_target_pairs={{0,32},{16,48},{32,0},{48,16},{64,96},{80,112},{96,64},{112,80},{1... | collective-permute-start | bytes 393224 | tf_op jit(solution)/shard_map/ppermute | solution.py:244
  73.3 6.3 %collective-permute-start.2 = (bf16[2,2,16,1024]{3,2,1,0:T(8,128)(2,1)S(1)}, bf16[2,2,16,1024]{3,2,1,0:T(8,128)(2,1)S(1)}, u32[]{:S(2)}, u32[]{:S(2)}) collective-permute-start(bf16[2,2,16,1024]{3,2,1,0:T(8,128)(2,1)S(1)} %add_convert_fusion.2), channel_id=1, source_target_pairs={{0,96},{16,112},{32,64},{48,80},{64,32},{80,48},{96,0},{112,16},{1... | collective-permute-start | bytes 393224 | tf_op jit(solution)/shard_map/ppermute | solution.py:244
  134.8 1.4 collective-permute-start.3
  136.3 5.6 %collective-permute-start.4 = (bf16[2,2,16,1024]{3,2,1,0:T(8,128)(2,1)S(1)}, bf16[2,2,16,1024]{3,2,1,0:T(8,128)(2,1)S(1)}, u32[]{:S(2)}, u32[]{:S(2)}) collective-permute-start(bf16[2,2,16,1024]{3,2,1,0:T(8,128)(2,1)S(1)} %add_convert_fusion.1), channel_id=1, source_target_pairs={{0,32},{16,48},{32,0},{48,16},{64,96},{80,112},{96,64},{112,80},{1... | collective-permute-start | bytes 393224 | tf_op jit(solution)/shard_map/ppermute | solution.py:244
  142.0 6.3 %collective-permute-start.5 = (bf16[2,2,16,1024]{3,2,1,0:T(8,128)(2,1)S(1)}, bf16[2,2,16,1024]{3,2,1,0:T(8,128)(2,1)S(1)}, u32[]{:S(2)}, u32[]{:S(2)}) collective-permute-start(bf16[2,2,16,1024]{3,2,1,0:T(8,128)(2,1)S(1)} %add_convert_fusion), channel_id=1, source_target_pairs={{0,96},{16,112},{32,64},{48,80},{64,32},{80,48},{96,0},{112,16},{1... | collective-permute-start | bytes 393224 | tf_op jit(solution)/shard_map/ppermute | solution.py:244
  148.3 30.1 %copy-start.2 = (f32[2,2,16,1024]{3,2,1,0:T(8,128)}, f32[2,2,16,1024]{3,2,1,0:T(8,128)S(1)}, u32[]{:S(2)}) copy-start(f32[2,2,16,1024]{3,2,1,0:T(8,128)S(1)} %multiply_subtract_fusion.model_ref) | copy-start | bytes 786436

commit v4 on v3

--- a/solution.py
+++ b/solution.py
@@ -106,8 +106,16 @@
     return held_ref
 
 
-def forward_kernel(model_ref, raw_ref, ranks_ref, out_ref, held_ref, wide_ref, sems):
+def first_kernel(source_ref, raw_ref, ranks_ref, out_ref, held_ref, wide_ref, sems, model_ref, model_sem):
+    copy = pltpu.make_async_copy(source_ref, model_ref, model_sem)
+    copy.start()
+    forward_kernel(model_ref, raw_ref, ranks_ref, out_ref, held_ref, wide_ref, sems, copy.wait)
+
+
+def forward_kernel(model_ref, raw_ref, ranks_ref, out_ref, held_ref, wide_ref, sems, ready=None):
     start_fetch(raw_ref, held_ref, sems)
+    if ready is not None:
+        ready()
     basis_ref = rows_by_pair(held_ref)
     _, first, rank = lane_facts()
     for j in range(4):
@@ -251,6 +259,12 @@
     right = pltpu.with_memory_space_constraint(right_bases, pltpu.HBM)
     ranks = tile_ranks.reshape(64, F)
     forward = call(forward_kernel, [VMEM, HBM, SMEM], PACKED, [HELD, wide(4), SEMS])
+    first = call(
+        first_kernel,
+        [HBM, HBM, SMEM],
+        PACKED,
+        [HELD, wide(4), SEMS, pltpu.VMEM((2, F, NV, 1024), jnp.float32), pltpu.SemaphoreType.DMA],
+    )
     middle = call(middle_kernel, [VMEM, HBM] + [VMEM] * 3, PACKED, [HELD, TOTAL, wide(), SEMS])
     last = call(
         last_kernel,
@@ -263,7 +277,11 @@
     )
     estimate = model_init
     for iteration in range(ITERS):
-        got = exchange(forward(estimate, right, ranks))
+        if iteration == 0:
+            sent = first(pltpu.with_memory_space_constraint(model_init, pltpu.HBM), right, ranks)
+        else:
+            sent = forward(estimate, right, ranks)
+        got = exchange(sent)
         back = exchange(middle(got, left, observed, gate_start, gate_stop))
         estimate = estimate - step_length * row_sum(gradient(back, right, ranks))
     got = exchange(forward(estimate, right, ranks))

time: 179 us -> 178 us (level)
    pallas_call x0 -> x2, Pallas kernels: none -> 16.2 us  [the longest x1 8.15 us: shards(): first(pltpu.with_memory_space_constraint(model_init, pltpu.HBM), right, r...]
    pallas_call x3 -> x1, Pallas kernels: 24.2 us -> 8.06 us  [shards(): got = exchange(forward(estimate, right, ranks))]
where the time goes in v4:
time: 178 us
  blocking collectives  85.1 us (48%)
  Pallas kernels  63.9 us (36%)
  waiting for transfers between devices  18.8 us (11%)
  starting transfers between devices  7.81 us (4%)
    all_to_all x5, blocking collectives, exchange(): return lax.all_to_all(parts, 'col', 0, 0, tiled=True).reshape(64, NV, WIDE)  85.1 us
    pallas_call x2, Pallas kernels, shards(): back = exchange(middle(got, left, observed, gate_start, gate_stop))  20.7 us
    ppermute x6, waiting for transfers between devices, row_sum(): lax.ppermute(low.astype(jnp.bfloat16), 'row', [(d, d ^ step) for d in ran...  18.8 us
    pallas_call x2, Pallas kernels, shards(): estimate = estimate - step_length * row_sum(gradient(back, right, ranks))  12.5 us
    pallas_call x1, Pallas kernels, shards(): first(pltpu.with_memory_space_constraint(model_init, pltpu.HBM), right, r...  8.15 us
    pallas_call x1, Pallas kernels, shards(): got = exchange(forward(estimate, right, ranks))  8.06 us
    pallas_call x1, Pallas kernels, shards(): sent = forward(estimate, right, ranks)  8.06 us
    ppermute x6, starting transfers between devices, row_sum(): lax.ppermute(low.astype(jnp.bfloat16), 'row', [(d, d ^ step) for d in ran...  7.81 us
  transfers between devices with their start and end apart: 6, of which 6 were waited for; matrix products, arithmetic and copies ran while one was open for 0% of the time, Pallas kernels for 0%

profile of v4, /device:TPU:0, one launch (start us, length us, event | category | flops | bytes accessed | tf_op | source)
XLA Modules:
  0.0 177.7 jit_solution(16552629590529372976)
XLA Ops:
  0.6 0.0 copy-start.3
  0.6 0.0 copy-start.2
  0.7 0.0 copy-start.1
  0.7 0.8 copy.21
  1.5 8.2 %first_kernel.1 = bf16[64,16,384]{2,1,0:T(8,128)(2,1)S(1)} custom-call(f32[2,2,16,1024]{3,2,1,0:T(8,128)} %source_ref.1, bf16[16,4,2,96,2,256]{5,4,3,2,1,0:T(2,128)(2,1)} %raw_ref.9, s32[64,2]{1,0:T(8,128)S(1)} %bitcast.22), custom_call_target="tpu_custom_call" | custom-call | tf_op jit(solution)/shard_map/first_kernel/pallas_call | solution.py:281
  9.6 22.3 %all_to_all.25 = bf16[16,4,16,384]{3,2,1,0:T(8,128)(2,1)S(1)} all-to-all(bf16[16,4,16,384]{3,2,1,0:T(8,128)(2,1)S(1)} %bitcast.20), channel_id=1, replica_groups=mesh['row'=8,'col'=16] {'col'}, dimensions={0} | all-to-all | bytes 1572864 | tf_op jit(solution)/shard_map/all_to_all | solution.py:246
  31.9 0.0 copy-done.3
  31.9 0.0 copy-done.2
  32.0 0.0 copy-done.1
  32.0 0.0 copy-start.4
  32.0 10.4 %middle_kernel.2 = bf16[64,16,384]{2,1,0:T(8,128)(2,1)S(1)} custom-call(bf16[64,16,384]{2,1,0:T(8,128)(2,1)S(1)} %bitcast.12, bf16[64,2,96,2,256]{4,3,2,1,0:T(2,128)(2,1)} %bitcast.27, f32[2,2,16,256]{3,2,1,0:T(8,128)S(1)} %copy-done.1, s32[16,256]{1,0:T(8,128)S(1)} %copy-done.2, s32[16,256]{1,0:T(8,128)S(1)} %copy-done.3), custom_call_target="tpu_custom_call" | custom-call | tf_op jit(solution)/shard_map/middle_kernel/pallas_call | solution.py:285
  42.3 16.7 %all_to_all.26 = bf16[16,4,16,384]{3,2,1,0:T(8,128)(2,1)S(1)} all-to-all(bf16[16,4,16,384]{3,2,1,0:T(8,128)(2,1)S(1)} %bitcast.13), channel_id=1, replica_groups=mesh['row'=8,'col'=16] {'col'}, dimensions={0} | all-to-all | bytes 1572864 | tf_op jit(solution)/shard_map/all_to_all | solution.py:246
  59.0 6.3 %gradient_kernel.2 = f32[2,2,16,1024]{3,2,1,0:T(8,128)S(1)} custom-call(bf16[64,16,384]{2,1,0:T(8,128)(2,1)S(1)} %bitcast.17, bf16[16,4,2,96,2,256]{5,4,3,2,1,0:T(2,128)(2,1)} %raw_ref.9, s32[64,2]{1,0:T(8,128)S(1)} %bitcast.23), custom_call_target="tpu_custom_call" | custom-call | tf_op jit(solution)/shard_map/gradient_kernel/pallas_call | solution.py:286
  65.3 0.1 collective-permute-start
  65.4 1.3 collective-permute-done
  66.8 1.6 collective-permute-start.1
  68.3 4.1 %collective-permute-done.1 = bf16[2,2,16,1024]{3,2,1,0:T(8,128)(2,1)S(1)} collective-permute-done((bf16[2,2,16,1024]{3,2,1,0:T(8,128)(2,1)S(1)}, bf16[2,2,16,1024]{3,2,1,0:T(8,128)(2,1)S(1)}, u32[]{:S(2)}, u32[]{:S(2)}) %collective-permute-start.1) | collective-permute-done | bytes 131104 | tf_op jit(solution)/shard_map/ppermute | solution.py:252
  72.4 2.8 %collective-permute-start.2 = (bf16[2,2,16,1024]{3,2,1,0:T(8,128)(2,1)S(1)}, bf16[2,2,16,1024]{3,2,1,0:T(8,128)(2,1)S(1)}, u32[]{:S(2)}, u32[]{:S(2)}) collective-permute-start(bf16[2,2,16,1024]{3,2,1,0:T(8,128)(2,1)S(1)} %add_convert_fusion.2), channel_id=1, source_target_pairs={{0,96},{16,112},{32,64},{48,80},{64,32},{80,48},{96,0},{112,16},{1... | collective-permute-start | bytes 393224 | tf_op jit(solution)/shard_map/ppermute | solution.py:252
  75.3 3.4 %collective-permute-done.2 = bf16[2,2,16,1024]{3,2,1,0:T(8,128)(2,1)S(1)} collective-permute-done((bf16[2,2,16,1024]{3,2,1,0:T(8,128)(2,1)S(1)}, bf16[2,2,16,1024]{3,2,1,0:T(8,128)(2,1)S(1)}, u32[]{:S(2)}, u32[]{:S(2)}) %collective-permute-start.2) | collective-permute-done | bytes 131104 | tf_op jit(solution)/shard_map/ppermute | solution.py:252
  78.7 0.0 copy-done.4
  78.7 8.1 %forward_kernel.2 = bf16[64,16,384]{2,1,0:T(8,128)(2,1)S(1)} custom-call(f32[2,2,16,1024]{3,2,1,0:T(8,128)S(1)} %multiply_subtract_fusion.1.model_ref, bf16[16,4,2,96,2,256]{5,4,3,2,1,0:T(2,128)(2,1)} %raw_ref.9, s32[64,2]{1,0:T(8,128)S(1)} %bitcast.24), custom_call_target="tpu_custom_call" | custom-call | tf_op jit(solution)/shard_map/forward_kernel/pallas_call | solution.py:283
  86.8 15.6 %all_to_all.27 = bf16[16,4,16,384]{3,2,1,0:T(8,128)(2,1)S(1)} all-to-all(bf16[16,4,16,384]{3,2,1,0:T(8,128)(2,1)S(1)} %bitcast.21), channel_id=1, replica_groups=mesh['row'=8,'col'=16] {'col'}, dimensions={0} | all-to-all | bytes 1572864 | tf_op jit(solution)/shard_map/all_to_all | solution.py:246
  102.5 10.3 %middle_kernel.3 = bf16[64,16,384]{2,1,0:T(8,128)(2,1)S(1)} custom-call(bf16[64,16,384]{2,1,0:T(8,128)(2,1)S(1)} %bitcast.14, bf16[64,2,96,2,256]{4,3,2,1,0:T(2,128)(2,1)} %bitcast.28, f32[2,2,16,256]{3,2,1,0:T(8,128)S(1)} %copy-done.1, s32[16,256]{1,0:T(8,128)S(1)} %copy-done.2, s32[16,256]{1,0:T(8,128)S(1)} %copy-done.3), custom_call_target="tpu_custom_call" | custom-call | tf_op jit(solution)/shard_map/middle_kernel/pallas_call | solution.py:285
  112.8 14.9 %all_to_all.28 = bf16[16,4,16,384]{3,2,1,0:T(8,128)(2,1)S(1)} all-to-all(bf16[16,4,16,384]{3,2,1,0:T(8,128)(2,1)S(1)} %bitcast.15), channel_id=1, replica_groups=mesh['row'=8,'col'=16] {'col'}, dimensions={0} | all-to-all | bytes 1572864 | tf_op jit(solution)/shard_map/all_to_all | solution.py:246
  127.7 6.3 %gradient_kernel.3 = f32[2,2,16,1024]{3,2,1,0:T(8,128)S(1)} custom-call(bf16[64,16,384]{2,1,0:T(8,128)(2,1)S(1)} %bitcast.18, bf16[16,4,2,96,2,256]{5,4,3,2,1,0:T(2,128)(2,1)} %raw_ref.9, s32[64,2]{1,0:T(8,128)S(1)} %bitcast.25), custom_call_target="tpu_custom_call" | custom-call | tf_op jit(solution)/shard_map/gradient_kernel/pallas_call | solution.py:286
  134.0 0.1 collective-permute-start.3
  134.1 1.3 collective-permute-done.3
  135.5 0.4 collective-permute-start.4
  135.8 5.3 %collective-permute-done.4 = bf16[2,2,16,1024]{3,2,1,0:T(8,128)(2,1)S(1)} collective-permute-done((bf16[2,2,16,1024]{3,2,1,0:T(8,128)(2,1)S(1)}, bf16[2,2,16,1024]{3,2,1,0:T(8,128)(2,1)S(1)}, u32[]{:S(2)}, u32[]{:S(2)}) %collective-permute-start.4) | collective-permute-done | bytes 131104 | tf_op jit(solution)/shard_map/ppermute | solution.py:252
  141.1 2.8 %collective-permute-start.5 = (bf16[2,2,16,1024]{3,2,1,0:T(8,128)(2,1)S(1)}, bf16[2,2,16,1024]{3,2,1,0:T(8,128)(2,1)S(1)}, u32[]{:S(2)}, u32[]{:S(2)}) collective-permute-start(bf16[2,2,16,1024]{3,2,1,0:T(8,128)(2,1)S(1)} %add_convert_fusion), channel_id=1, source_target_pairs={{0,96},{16,112},{32,64},{48,80},{64,32},{80,48},{96,0},{112,16},{1... | collective-permute-start | bytes 393224 | tf_op jit(solution)/shard_map/ppermute | solution.py:252
  144.0 3.4 %collective-permute-done.5 = bf16[2,2,16,1024]{3,2,1,0:T(8,128)(2,1)S(1)} collective-permute-done((bf16[2,2,16,1024]{3,2,1,0:T(8,128)(2,1)S(1)}, bf16[2,2,16,1024]{3,2,1,0:T(8,128)(2,1)S(1)}, u32[]{:S(2)}, u32[]{:S(2)}) %collective-permute-start.5) | collective-permute-done | bytes 131104 | tf_op jit(solution)/shard_map/ppermute | solution.py:252
  147.4 0.0 copy-start
  147.5 8.1 %forward_kernel.3 = bf16[64,16,384]{2,1,0:T(8,128)(2,1)S(1)} custom-call(f32[2,2,16,1024]{3,2,1,0:T(8,128)S(1)} %multiply_subtract_fusion.model_ref, bf16[16,4,2,96,2,256]{5,4,3,2,1,0:T(2,128)(2,1)} %raw_ref.9, s32[64,2]{1,0:T(8,128)S(1)} %bitcast.26), custom_call_target="tpu_custom_call" | custom-call | tf_op jit(solution)/shard_map/forward_kernel/pallas_call | solution.py:287
  155.5 15.6 %all_to_all.29 = bf16[16,4,16,384]{3,2,1,0:T(8,128)(2,1)S(1)} all-to-all(bf16[16,4,16,384]{3,2,1,0:T(8,128)(2,1)S(1)} %bitcast.19), channel_id=1, replica_groups=mesh['row'=8,'col'=16] {'col'}, dimensions={0} | all-to-all | bytes 1572864 | tf_op jit(solution)/shard_map/all_to_all | solution.py:246
  171.1 6.4 %last_kernel.1 = f32[2,2,16,256]{3,2,1,0:T(8,128)} custom-call(bf16[64,16,384]{2,1,0:T(8,128)(2,1)S(1)} %bitcast.16, bf16[64,2,96,2,256]{4,3,2,1,0:T(2,128)(2,1)} %bitcast.29, f32[2,2,16,256]{3,2,1,0:T(8,128)S(1)} %copy-done.1, s32[16,256]{1,0:T(8,128)S(1)} %copy-done.2, s32[16,256]{1,0:T(8,128)S(1)} %copy-done.3), custom_call_target="tpu_custom_call" | custom-call | tf_op jit(solution)/shard_map/last_kernel/pallas_call | solution.py:288
  177.5 0.0 copy-done
  (8 shorter events, 0.2 us)
Async XLA Ops:
  0.6 31.3 %copy-start.3 = (s32[16,256]{1,0:T(8,128)S(1)}, s32[16,256]{1,0:T(8,128)}, u32[]{:S(2)}) copy-start(s32[16,256]{1,0:T(8,128)} %stop_ref.5) | copy-start | bytes 49156
  0.6 31.3 %copy-start.2 = (s32[16,256]{1,0:T(8,128)S(1)}, s32[16,256]{1,0:T(8,128)}, u32[]{:S(2)}) copy-start(s32[16,256]{1,0:T(8,128)} %start_ref.5) | copy-start | bytes 49156
  0.7 31.3 %copy-start.1 = (f32[2,2,16,256]{3,2,1,0:T(8,128)S(1)}, f32[2,2,16,256]{3,2,1,0:T(8,128)}, u32[]{:S(2)}) copy-start(f32[2,2,16,256]{3,2,1,0:T(8,128)} %observed_ref.5) | copy-start | bytes 196612
  32.0 46.7 %copy-start.4 = (f32[2,2,16,1024]{3,2,1,0:T(8,128)S(1)}, f32[2,2,16,1024]{3,2,1,0:T(8,128)}, u32[]{:S(2)}) copy-start(f32[2,2,16,1024]{3,2,1,0:T(8,128)} %source_ref.1) | copy-start | bytes 786436
  65.3 1.4 collective-permute-start
  66.8 5.6 %collective-permute-start.1 = (bf16[2,2,16,1024]{3,2,1,0:T(8,128)(2,1)S(1)}, bf16[2,2,16,1024]{3,2,1,0:T(8,128)(2,1)S(1)}, u32[]{:S(2)}, u32[]{:S(2)}) collective-permute-start(bf16[2,2,16,1024]{3,2,1,0:T(8,128)(2,1)S(1)} %add_convert_fusion.3), channel_id=1, source_target_pairs={{0,32},{16,48},{32,0},{48,16},{64,96},{80,112},{96,64},{112,80},{1... | collective-permute-start | bytes 393224 | tf_op jit(solution)/shard_map/ppermute | solution.py:252
  72.4 6.3 %collective-permute-start.2 = (bf16[2,2,16,1024]{3,2,1,0:T(8,128)(2,1)S(1)}, bf16[2,2,16,1024]{3,2,1,0:T(8,128)(2,1)S(1)}, u32[]{:S(2)}, u32[]{:S(2)}) collective-permute-start(bf16[2,2,16,1024]{3,2,1,0:T(8,128)(2,1)S(1)} %add_convert_fusion.2), channel_id=1, source_target_pairs={{0,96},{16,112},{32,64},{48,80},{64,32},{80,48},{96,0},{112,16},{1... | collective-permute-start | bytes 393224 | tf_op jit(solution)/shard_map/ppermute | solution.py:252
  134.0 1.4 collective-permute-start.3
  135.5 5.6 %collective-permute-start.4 = (bf16[2,2,16,1024]{3,2,1,0:T(8,128)(2,1)S(1)}, bf16[2,2,16,1024]{3,2,1,0:T(8,128)(2,1)S(1)}, u32[]{:S(2)}, u32[]{:S(2)}) collective-permute-start(bf16[2,2,16,1024]{3,2,1,0:T(8,128)(2,1)S(1)} %add_convert_fusion.1), channel_id=1, source_target_pairs={{0,32},{16,48},{32,0},{48,16},{64,96},{80,112},{96,64},{112,80},{1... | collective-permute-start | bytes 393224 | tf_op jit(solution)/shard_map/ppermute | solution.py:252
  141.1 6.3 %collective-permute-start.5 = (bf16[2,2,16,1024]{3,2,1,0:T(8,128)(2,1)S(1)}, bf16[2,2,16,1024]{3,2,1,0:T(8,128)(2,1)S(1)}, u32[]{:S(2)}, u32[]{:S(2)}) collective-permute-start(bf16[2,2,16,1024]{3,2,1,0:T(8,128)(2,1)S(1)} %add_convert_fusion), channel_id=1, source_target_pairs={{0,96},{16,112},{32,64},{48,80},{64,32},{80,48},{96,0},{112,16},{1... | collective-permute-start | bytes 393224 | tf_op jit(solution)/shard_map/ppermute | solution.py:252
  147.4 30.1 %copy-start = (f32[2,2,16,1024]{3,2,1,0:T(8,128)}, f32[2,2,16,1024]{3,2,1,0:T(8,128)S(1)}, u32[]{:S(2)}) copy-start(f32[2,2,16,1024]{3,2,1,0:T(8,128)S(1)} %multiply_subtract_fusion.model_ref) | copy-start | bytes 786436
